TPU v7x, 32 devices: a whole 2x2x4 slice. The times are simulated.
32 devices in a mesh: orb: 8 (over y, x, core), slab: 4 (over z).
Axes of the slice: x: 2, y: 2, z: 4, core: 2. Of those that a mesh axis runs over, the one named last changes fastest.
Arguments:
- orbitals: float32 [8, 2, 128, 32, 128], P('orb', None, None, 'slab'), may hold values from -7 to 7, as said below
- potential: float32 [128, 32, 128], P(None, 'slab'), may hold values from 0 to 2
- occupation: float32 [8], P('orb'), may hold values from 0.5 to 2
- e_field: float32 [3, 128, 32, 128], P(None, 'orb', 'slab'), may hold values from -3 to 3
- a_field: float32 [3, 128, 32, 128], P(None, 'orb', 'slab'), may hold values from -1.8 to 1.8
Outputs:
- orbitals_next: float32 [8, 2, 128, 32, 128], P('orb', None, None, 'slab')
- electric_field: float32 [3, 128, 32, 128], P(None, 'orb', 'slab')
- vector_potential: float32 [3, 128, 32, 128], P(None, 'orb', 'slab')
Inputs may be any that keep to these rules, and one draw needn't show every extreme that they name: `orbitals`: real and imaginary parts of each orbital at each cell.
All inputs are finite; a program needn't handle non-finite values.
Results may differ from a plain program's by a relative error of at most 0.0003.
Values sent between devices are 32-bit elements; how exact they have to be, the bound alone decides.
A program may use at most 64 MiB of HBM per device.

v0:
```python
import jax
import jax.numpy as jnp
from jax import lax
from jax.sharding import PartitionSpec as P

TERMS = 4
STEPS = 2


time_step = 0.3
wave_step = 0.5
epsilon = 1e-06


def extended(shard, sides, width):
    for axis, dim in sides:
        size, length = (lax.axis_size(axis), shard.shape[dim])
        up = [(i, (i + 1) % size) for i in range(size - 1)]
        down = [(j, i) for i, j in up]
        last = lax.slice_in_dim(shard, length - width, length, axis=dim)
        leading = lax.slice_in_dim(shard, 0, width, axis=dim)
        before = lax.ppermute(last, axis, up)
        after = lax.ppermute(leading, axis, down)
        shard = jnp.concatenate([before, shard, after], axis=dim)
    return shard


def trim_axis(array, axis, start, stop):
    return lax.slice_in_dim(array, start, array.shape[axis] + stop, axis=axis)


def next_lane(array):
    edge = jnp.zeros(array.shape[:-1] + (1,), array.dtype)
    return jnp.concatenate([array[..., 1:], edge], axis=-1)


def prev_lane(array):
    edge = jnp.zeros(array.shape[:-1] + (1,), array.dtype)
    return jnp.concatenate([edge, array[..., :-1]], axis=-1)


def forward(field, axis):
    if axis == 2:
        diff = next_lane(field) - field
    else:
        diff = trim_axis(field, axis, 1, 0) - trim_axis(field, axis, 0, -1)
    for other in (0, 1):
        if other != axis:
            diff = trim_axis(diff, other, 0, -1)
    return diff


def backward(field, axis, edge):
    if axis == 2:
        diff = field - jnp.concatenate([edge, field[..., :-1]], axis=-1)
    else:
        diff = trim_axis(field, axis, 1, 0) - trim_axis(field, axis, 0, -1)
    for other in (0, 1):
        if other != axis:
            diff = trim_axis(diff, other, 1, 0)
    return diff


def double_curl(padded):
    comp_x, comp_y, comp_z = (padded[0], padded[1], padded[2])
    inner_x = forward(comp_z, 2) - forward(comp_y, 1)
    inner_y = forward(comp_x, 1) - forward(comp_z, 0)
    inner_z = forward(comp_y, 0) - forward(comp_x, 2)
    edge_x = comp_z[1:, 1:, 0:1] * 0.0 + comp_z[:-1, :-1, 0:1]
    edge_z = -comp_x[:-1, :-1, 0:1]
    out_x = backward(inner_z, 2, edge_z) - backward(inner_y, 1, None)
    out_y = backward(inner_x, 1, None) - backward(inner_z, 0, None)
    out_z = backward(inner_y, 0, None) - backward(inner_x, 2, edge_x)
    return jnp.stack([out_x, out_y, out_z])


def neighbours(padded):
    center = padded[:, :, 1:-1, 1:-1, :]
    x_plus = padded[:, :, 2:, 1:-1, :]
    x_minus = padded[:, :, :-2, 1:-1, :]
    z_plus = padded[:, :, 1:-1, 2:, :]
    z_minus = padded[:, :, 1:-1, :-2, :]
    y_plus = next_lane(center)
    y_minus = prev_lane(center)
    return (center, (x_plus, x_minus), (y_plus, y_minus), (z_plus, z_minus))


def hamiltonian(padded, field, weight):
    center, along_x, along_y, along_z = neighbours(padded)
    laplace = (
        along_x[0] + along_x[1] + along_y[0] + along_y[1] + along_z[0] + along_z[1] - 6.0 * center
    )
    drift = 0.5 * (
        field[0] * (along_x[0] - along_x[1])
        + field[1] * (along_y[0] - along_y[1])
        + field[2] * (along_z[0] - along_z[1])
    )
    real_h = -0.5 * laplace[:, 0] + drift[:, 1] + weight * center[:, 0]
    imag_h = -0.5 * laplace[:, 1] - drift[:, 0] + weight * center[:, 1]
    return (real_h, imag_h)


def taylor_term(real_h, imag_h, order):
    factor = time_step / order
    return jnp.stack([factor * imag_h, -factor * real_h], axis=1)


def current_density(padded, field, weights):
    center, along_x, along_y, along_z = neighbours(padded)
    real_c = center[:, 0]
    imag_c = center[:, 1]
    density = real_c * real_c + imag_c * imag_c
    parts = []
    for pair, comp in ((along_x, 0), (along_y, 1), (along_z, 2)):
        grad_r = 0.5 * (pair[0][:, 0] - pair[1][:, 0])
        grad_i = 0.5 * (pair[0][:, 1] - pair[1][:, 1])
        flow = real_c * grad_i - imag_c * grad_r + field[comp] * density
        parts.append(jnp.sum(weights[:, None, None, None] * flow, axis=0))
    return jnp.stack(parts)


def pad_plane(array):
    return jnp.pad(array, ((0, 0), (0, 0), (1, 1), (0, 0), (0, 0)))


def propagate(orbitals, field, weight):
    total = orbitals
    term = orbitals
    for order in range(1, TERMS + 1):
        rim = extended(term, (("slab", 3),), 1)
        real_h, imag_h = hamiltonian(pad_plane(rim), field, weight)
        term = taylor_term(real_h, imag_h, order)
        total = total + term
    return total


def per_device(orbitals, potential, occupation, e_field, a_field):
    slabs = lax.axis_size("slab")
    cells = orbitals.shape[2] * orbitals.shape[3] * orbitals.shape[4] * slabs
    orbs_total = orbitals.shape[0] * lax.axis_size("orb")
    weights = occupation * (1.0 / orbs_total)
    a_state = a_field
    e_state = e_field
    for step in range(STEPS):
        field = lax.all_gather(a_state, "orb", axis=1, tiled=True)
        weight = potential + 0.5 * jnp.sum(field * field, axis=0)
        moved = propagate(orbitals, field, weight)
        local_norm = jnp.sum(moved * moved, axis=(1, 2, 3, 4))
        norm = lax.psum(local_norm, "slab")
        scale = (1.0 / jnp.sqrt(norm / cells + epsilon))[:, None, None, None, None]
        rim = extended(moved, (("slab", 3),), 1)
        flow = current_density(pad_plane(rim) * scale, field, weights)
        orbitals = moved * scale
        total_flow = lax.psum_scatter(flow, "orb", scatter_dimension=1, tiled=True)
        padded_field = extended(a_state, (("orb", 1), ("slab", 2)), 1)
        e_state = e_state + wave_step * (double_curl(padded_field) - total_flow)
        a_state = a_state - wave_step * e_state
    return (orbitals, e_state, a_state)


def solution(mesh):
    return jax.shard_map(
        per_device,
        mesh=mesh,
        in_specs=(
            P("orb", None, None, "slab", None),
            P(None, "slab", None),
            P("orb"),
            P(None, "orb", "slab", None),
            P(None, "orb", "slab", None),
        ),
        out_specs=(
            P("orb", None, None, "slab", None),
            P(None, "orb", "slab", None),
            P(None, "orb", "slab", None),
        ),
        check_vma=False,
    )
```

profile of v0, /device:TPU:0, one launch (start us, length us, event | category | flops | bytes accessed | tf_op | source)
XLA Modules:
  0.0 272.4 jit_solution(9545134804376292991)
XLA Ops:
  8.7 2.4 collective-permute-start.10
  11.1 1.7 fusion.173
  12.8 1.3 collective-permute-start.1
  14.1 4.9 %collective-permute-start = (f32[1,2,128,1,128]{4,3,2,1,0:T(1,128)S(1)}, f32[1,2,128,1,128]{4,3,2,1,0:T(1,128)S(1)}, u32[]{:S(2)}, u32[]{:S(2)}) collective-permute-start(f32[1,2,128,1,128]{4,3,2,1,0:T(1,128)S(1)} %get-tuple-element.73), channel_id=1, source_target_pairs={{0,1},{1,2},{2,3},{4,5},{5,6},{6,7},{8,9},{9,10},{10,11},{12,13},{... | collective-permute-start | bytes 393224 | tf_op jit(solution)/shard_map/ppermute | solution.py:22
  19.1 1.3 collective-permute-start.11
  20.4 0.9 constant_dynamic-update-slice_fusion.1
  21.3 2.0 collective-permute-done.11
  23.3 1.3 collective-permute-start.13
  24.6 4.5 %collective-permute-start.12 = (f32[3,18,1,128]{3,2,1,0:T(1,128)S(1)}, f32[3,18,1,128]{3,2,1,0:T(1,128)S(1)}, u32[]{:S(2)}, u32[]{:S(2)}) collective-permute-start(f32[3,18,1,128]{3,2,1,0:T(1,128)S(1)} %get-tuple-element.87), channel_id=1, source_target_pairs={{0,1},{1,2},{2,3},{4,5},{5,6},{6,7},{8,9},{9,10},{10,11},{12,13},{... | collective-permute-start | bytes 82952 | tf_op jit(solution)/shard_map/ppermute | solution.py:22
  33.2 1.8 multiply_subtract_fusion.7
  35.1 3.2 %all-gather.3.cloned.1.call-done = f32[3,128,8,128]{3,2,1,0:T(8,128)} async-done(((f32[3,16,8,128]{3,2,1,0:T(8,128)}), f32[3,128,8,128]{3,2,1,0:T(8,128)}) %all-gather.3.cloned.1.call-update) | async-done | bytes 1572880 | tf_op jit(solution)/shard_map/all_gather | solution.py:145
  38.3 1.6 slice_bitcast_fusion.7
  40.8 0.9 add_multiply_fusion.7
  42.6 1.3 collective-permute-start.3
  43.9 4.6 %collective-permute-start.2 = (f32[1,2,128,1,128]{4,3,2,1,0:T(1,128)S(1)}, f32[1,2,128,1,128]{4,3,2,1,0:T(1,128)S(1)}, u32[]{:S(2)}, u32[]{:S(2)}) collective-permute-start(f32[1,2,128,1,128]{4,3,2,1,0:T(1,128)S(1)} %get-tuple-element.69), channel_id=1, source_target_pairs={{0,1},{1,2},{2,3},{4,5},{5,6},{6,7},{8,9},{9,10},{10,11},{12,13},{... | collective-permute-start | bytes 393224 | tf_op jit(solution)/shard_map/ppermute | solution.py:22
  48.8 1.3 collective-permute-done.3
  50.2 1.2 collective-permute-done.2
  51.7 0.8 add_multiply_fusion.6
  53.9 1.3 collective-permute-start.5
  55.2 5.0 %collective-permute-start.4 = (f32[1,2,128,1,128]{4,3,2,1,0:T(1,128)S(1)}, f32[1,2,128,1,128]{4,3,2,1,0:T(1,128)S(1)}, u32[]{:S(2)}, u32[]{:S(2)}) collective-permute-start(f32[1,2,128,1,128]{4,3,2,1,0:T(1,128)S(1)} %get-tuple-element.65), channel_id=1, source_target_pairs={{0,1},{1,2},{2,3},{4,5},{5,6},{6,7},{8,9},{9,10},{10,11},{12,13},{... | collective-permute-start | bytes 393224 | tf_op jit(solution)/shard_map/ppermute | solution.py:22
  61.2 1.5 collective-permute-done.4
  63.0 0.8 add_multiply_fusion.5
  65.0 1.3 collective-permute-start.7
  66.3 5.2 %collective-permute-start.6 = (f32[1,2,128,1,128]{4,3,2,1,0:T(1,128)S(1)}, f32[1,2,128,1,128]{4,3,2,1,0:T(1,128)S(1)}, u32[]{:S(2)}, u32[]{:S(2)}) collective-permute-start(f32[1,2,128,1,128]{4,3,2,1,0:T(1,128)S(1)} %get-tuple-element.61), channel_id=1, source_target_pairs={{0,1},{1,2},{2,3},{4,5},{5,6},{6,7},{8,9},{9,10},{10,11},{12,13},{... | collective-permute-start | bytes 393224 | tf_op jit(solution)/shard_map/ppermute | solution.py:22
  72.3 1.5 collective-permute-done.6
  74.2 0.9 add_multiply_fusion.4
  76.3 1.0 multiply_reduce_fusion.3
  77.4 1.3 collective-permute-start.15
  78.7 5.0 %collective-permute-start.14 = (f32[1,2,128,1,128]{4,3,2,1,0:T(1,128)S(1)}, f32[1,2,128,1,128]{4,3,2,1,0:T(1,128)S(1)}, u32[]{:S(2)}, u32[]{:S(2)}) collective-permute-start(f32[1,2,128,1,128]{4,3,2,1,0:T(1,128)S(1)} %get-tuple-element.53), channel_id=1, source_target_pairs={{0,1},{1,2},{2,3},{4,5},{5,6},{6,7},{8,9},{9,10},{10,11},{12,13},{... | collective-permute-start | bytes 393224 | tf_op jit(solution)/shard_map/ppermute | solution.py:22
  83.7 11.3 %psum.14 = f32[1]{0:T(128)} all-reduce(f32[1]{0:T(128)} %bitcast.29), channel_id=1, replica_groups=mesh['orb'=8,'slab'=4] {'slab'}, use_global_device_ids=true, to_apply=%region_2.3 | all-reduce | flops 1 | bytes 8 | tf_op jit(solution)/shard_map/psum | solution.py:149
  96.6 1.0 copy-done.4
  98.9 1.4 copy.27
  101.4 34.9 %reduce-scatter.9.cloned.1.call-done = f32[16,3072]{1,0:T(8,128)} async-done(((f32[128,3072]{1,0:T(8,128)}), f32[16,3072]{1,0:T(8,128)}) %reduce-scatter.9.cloned.1.call-update) | async-done | bytes 196624
  136.3 1.0 copy.13
  139.0 1.4 collective-permute-start.9
  140.4 4.6 %collective-permute-start.8 = (f32[1,2,128,1,128]{4,3,2,1,0:T(1,128)S(1)}, f32[1,2,128,1,128]{4,3,2,1,0:T(1,128)S(1)}, u32[]{:S(2)}, u32[]{:S(2)}) collective-permute-start(f32[1,2,128,1,128]{4,3,2,1,0:T(1,128)S(1)} %get-tuple-element.57), channel_id=1, source_target_pairs={{0,1},{1,2},{2,3},{4,5},{5,6},{6,7},{8,9},{9,10},{10,11},{12,13},{... | collective-permute-start | bytes 393224 | tf_op jit(solution)/shard_map/ppermute | solution.py:22
  145.3 1.3 collective-permute-start.23
  146.6 3.0 %collective-permute-start.22 = (f32[3,1,8,128]{3,2,1,0:T(8,128)S(1)}, f32[3,1,8,128]{3,2,1,0:T(8,128)S(1)}, u32[]{:S(2)}, u32[]{:S(2)}) collective-permute-start(f32[3,1,8,128]{3,2,1,0:T(8,128)S(1)} %get-tuple-element.89), channel_id=1, source_target_pairs={{0,4},{4,8},{8,12},{12,16},{16,20},{20,24},{24,28},{1,5},{5,9},{9,... | collective-permute-start | bytes 36872 | tf_op jit(solution)/shard_map/ppermute | solution.py:22
  150.5 1.3 collective-permute-start.25
  151.8 4.5 %collective-permute-start.24 = (f32[3,18,1,128]{3,2,1,0:T(1,128)S(1)}, f32[3,18,1,128]{3,2,1,0:T(1,128)S(1)}, u32[]{:S(2)}, u32[]{:S(2)}) collective-permute-start(f32[3,18,1,128]{3,2,1,0:T(1,128)S(1)} %get-tuple-element.85), channel_id=1, source_target_pairs={{0,1},{1,2},{2,3},{4,5},{5,6},{6,7},{8,9},{9,10},{10,11},{12,13},{... | collective-permute-start | bytes 82952 | tf_op jit(solution)/shard_map/ppermute | solution.py:22
  161.0 3.5 %all-gather.5.cloned.1.call-done = f32[3,128,8,128]{3,2,1,0:T(8,128)} async-done(((f32[3,16,8,128]{3,2,1,0:T(8,128)}), f32[3,128,8,128]{3,2,1,0:T(8,128)}) %all-gather.5.cloned.1.call-update) | async-done | bytes 1572880 | tf_op jit(solution)/shard_map/all_gather | solution.py:145
  164.5 1.6 slice_bitcast_fusion.4
  166.2 1.7 multiply_reduce_fusion
  168.0 0.9 add_multiply_fusion.3
  169.5 1.3 collective-permute-start.17
  170.8 4.8 %collective-permute-start.16 = (f32[1,2,128,1,128]{4,3,2,1,0:T(1,128)S(1)}, f32[1,2,128,1,128]{4,3,2,1,0:T(1,128)S(1)}, u32[]{:S(2)}, u32[]{:S(2)}) collective-permute-start(f32[1,2,128,1,128]{4,3,2,1,0:T(1,128)S(1)} %get-tuple-element.51), channel_id=1, source_target_pairs={{0,1},{1,2},{2,3},{4,5},{5,6},{6,7},{8,9},{9,10},{10,11},{12,13},{... | collective-permute-start | bytes 393224 | tf_op jit(solution)/shard_map/ppermute | solution.py:22
  175.9 1.1 collective-permute-done.17
  177.0 1.2 collective-permute-done.16
  178.6 0.8 add_multiply_fusion.2
  180.8 1.3 collective-permute-start.19
  182.1 5.0 %collective-permute-start.18 = (f32[1,2,128,1,128]{4,3,2,1,0:T(1,128)S(1)}, f32[1,2,128,1,128]{4,3,2,1,0:T(1,128)S(1)}, u32[]{:S(2)}, u32[]{:S(2)}) collective-permute-start(f32[1,2,128,1,128]{4,3,2,1,0:T(1,128)S(1)} %get-tuple-element.47), channel_id=1, source_target_pairs={{0,1},{1,2},{2,3},{4,5},{5,6},{6,7},{8,9},{9,10},{10,11},{12,13},{... | collective-permute-start | bytes 393224 | tf_op jit(solution)/shard_map/ppermute | solution.py:22
  188.1 1.5 collective-permute-done.18
  191.9 1.3 collective-permute-start.21
  193.2 5.0 %collective-permute-start.20 = (f32[1,2,128,1,128]{4,3,2,1,0:T(1,128)S(1)}, f32[1,2,128,1,128]{4,3,2,1,0:T(1,128)S(1)}, u32[]{:S(2)}, u32[]{:S(2)}) collective-permute-start(f32[1,2,128,1,128]{4,3,2,1,0:T(1,128)S(1)} %get-tuple-element.43), channel_id=1, source_target_pairs={{0,1},{1,2},{2,3},{4,5},{5,6},{6,7},{8,9},{9,10},{10,11},{12,13},{... | collective-permute-start | bytes 393224 | tf_op jit(solution)/shard_map/ppermute | solution.py:22
  199.2 1.5 collective-permute-done.20
  203.1 1.1 multiply_reduce_fusion.2
  204.3 1.3 collective-permute-start.27
  205.6 5.0 %collective-permute-start.26 = (f32[1,2,128,1,128]{4,3,2,1,0:T(1,128)S(1)}, f32[1,2,128,1,128]{4,3,2,1,0:T(1,128)S(1)}, u32[]{:S(2)}, u32[]{:S(2)}) collective-permute-start(f32[1,2,128,1,128]{4,3,2,1,0:T(1,128)S(1)} %get-tuple-element.39), channel_id=1, source_target_pairs={{0,1},{1,2},{2,3},{4,5},{5,6},{6,7},{8,9},{9,10},{10,11},{12,13},{... | collective-permute-start | bytes 393224 | tf_op jit(solution)/shard_map/ppermute | solution.py:22
  211.3 11.5 %psum.15 = f32[1]{0:T(128)} all-reduce(f32[1]{0:T(128)} %bitcast.65), channel_id=1, replica_groups=mesh['orb'=8,'slab'=4] {'slab'}, use_global_device_ids=true, to_apply=%region_6.7 | all-reduce | flops 1 | bytes 8 | tf_op jit(solution)/shard_map/psum | solution.py:149
  224.3 1.0 copy-done.5
  226.6 1.4 copy.26
  229.3 1.0 broadcast_multiply_fusion
  230.3 33.7 %reduce-scatter.11.cloned.1.call-done = f32[16,3072]{1,0:T(8,128)} async-done(((f32[128,3072]{1,0:T(8,128)}), f32[16,3072]{1,0:T(8,128)}) %reduce-scatter.11.cloned.1.call-update) | async-done | bytes 196624
  264.0 1.0 copy.15
  (221 shorter events, 38.4 us)
Async XLA Ops:
  7.2 22.0 %copy-start = (f32[1,2,128,8,128]{4,3,2,1,0:T(8,128)S(1)}, f32[1,2,128,8,128]{4,3,2,1,0:T(8,128)}, u32[]{:S(2)}) copy-start(f32[1,2,128,8,128]{4,3,2,1,0:T(8,128)} %param.5) | copy-start | bytes 3145732
  7.2 31.1 %all-gather.3.cloned.1.call-start = ((), (), s32[]{:S(2)}) async-start(), calls=%async_computation.2 | async-start | bytes 1769472 | tf_op jit(solution)/shard_map/all_gather | solution.py:145
  7.9 128.4 %reduce-scatter.9.cloned.1.call-start = ((), (), s32[]{:S(2)}) async-start(), calls=%async_computation.4 | async-start | bytes 1769472
  8.7 11.7 %collective-permute-start.10 = (f32[3,1,8,128]{3,2,1,0:T(8,128)S(1)}, f32[3,1,8,128]{3,2,1,0:T(8,128)S(1)}, u32[]{:S(2)}, u32[]{:S(2)}) collective-permute-start(f32[3,1,8,128]{3,2,1,0:T(8,128)S(1)} %get-tuple-element.92), channel_id=1, source_target_pairs={{0,4},{4,8},{8,12},{12,16},{16,20},{20,24},{24,28},{1,5},{5,9},{9,... | collective-permute-start | bytes 36872 | tf_op jit(solution)/shard_map/ppermute | solution.py:22
  12.8 19.7 %collective-permute-start.1 = (f32[1,2,128,1,128]{4,3,2,1,0:T(1,128)S(1)}, f32[1,2,128,1,128]{4,3,2,1,0:T(1,128)S(1)}, u32[]{:S(2)}, u32[]{:S(2)}) collective-permute-start(f32[1,2,128,1,128]{4,3,2,1,0:T(1,128)S(1)} %get-tuple-element.74), channel_id=1, source_target_pairs={{1,0},{2,1},{3,2},{5,4},{6,5},{7,6},{9,8},{10,9},{11,10},{13,12},{... | collective-permute-start | bytes 393224 | tf_op jit(solution)/shard_map/ppermute | solution.py:23
  14.1 18.4 %collective-permute-start = (f32[1,2,128,1,128]{4,3,2,1,0:T(1,128)S(1)}, f32[1,2,128,1,128]{4,3,2,1,0:T(1,128)S(1)}, u32[]{:S(2)}, u32[]{:S(2)}) collective-permute-start(f32[1,2,128,1,128]{4,3,2,1,0:T(1,128)S(1)} %get-tuple-element.73), channel_id=1, source_target_pairs={{0,1},{1,2},{2,3},{4,5},{5,6},{6,7},{8,9},{9,10},{10,11},{12,13},{... | collective-permute-start | bytes 393224 | tf_op jit(solution)/shard_map/ppermute | solution.py:22
  19.1 4.2 %collective-permute-start.11 = (f32[3,1,8,128]{3,2,1,0:T(8,128)S(1)}, f32[3,1,8,128]{3,2,1,0:T(8,128)S(1)}, u32[]{:S(2)}, u32[]{:S(2)}) collective-permute-start(f32[3,1,8,128]{3,2,1,0:T(8,128)S(1)} %get-tuple-element.91), channel_id=1, source_target_pairs={{4,0},{8,4},{12,8},{16,12},{20,16},{24,20},{28,24},{5,1},{9,5},{13... | collective-permute-start | bytes 36872 | tf_op jit(solution)/shard_map/ppermute | solution.py:23
  23.3 6.9 %collective-permute-start.13 = (f32[3,18,1,128]{3,2,1,0:T(1,128)S(1)}, f32[3,18,1,128]{3,2,1,0:T(1,128)S(1)}, u32[]{:S(2)}, u32[]{:S(2)}) collective-permute-start(f32[3,18,1,128]{3,2,1,0:T(1,128)S(1)} %get-tuple-element.88), channel_id=1, source_target_pairs={{1,0},{2,1},{3,2},{5,4},{6,5},{7,6},{9,8},{10,9},{11,10},{13,12},{... | collective-permute-start | bytes 82952 | tf_op jit(solution)/shard_map/ppermute | solution.py:23
  24.6 6.1 %collective-permute-start.12 = (f32[3,18,1,128]{3,2,1,0:T(1,128)S(1)}, f32[3,18,1,128]{3,2,1,0:T(1,128)S(1)}, u32[]{:S(2)}, u32[]{:S(2)}) collective-permute-start(f32[3,18,1,128]{3,2,1,0:T(1,128)S(1)} %get-tuple-element.87), channel_id=1, source_target_pairs={{0,1},{1,2},{2,3},{4,5},{5,6},{6,7},{8,9},{9,10},{10,11},{12,13},{... | collective-permute-start | bytes 82952 | tf_op jit(solution)/shard_map/ppermute | solution.py:22
  29.5 3.4 %copy-start.11 = (f32[1,2,128,8,127]{4,3,2,1,0:T(8,128)}, f32[1,2,128,8,127]{4,3,2,1,0:T(8,128)S(1)}, u32[]{:S(2)}) copy-start(f32[1,2,128,8,127]{4,3,2,1,0:T(8,128)S(1)} %get-tuple-element.71) | copy-start | bytes 3121156
  29.5 3.4 %copy-start.13 = (f32[1,2,128,8,127]{4,3,2,1,0:T(8,128)}, f32[1,2,128,8,127]{4,3,2,1,0:T(8,128)S(1)}, u32[]{:S(2)}) copy-start(f32[1,2,128,8,127]{4,3,2,1,0:T(8,128)S(1)} %get-tuple-element.72) | copy-start | bytes 3121156
  38.3 1.9 copy-start.3
  38.3 2.2 copy-start.12
  38.3 2.5 copy-start.14
  38.3 2.5 copy-start.31
  38.3 2.5 copy-start.35
  42.6 7.5 %collective-permute-start.3 = (f32[1,2,128,1,128]{4,3,2,1,0:T(1,128)S(1)}, f32[1,2,128,1,128]{4,3,2,1,0:T(1,128)S(1)}, u32[]{:S(2)}, u32[]{:S(2)}) collective-permute-start(f32[1,2,128,1,128]{4,3,2,1,0:T(1,128)S(1)} %get-tuple-element.70), channel_id=1, source_target_pairs={{1,0},{2,1},{3,2},{5,4},{6,5},{7,6},{9,8},{10,9},{11,10},{13,12},{... | collective-permute-start | bytes 393224 | tf_op jit(solution)/shard_map/ppermute | solution.py:23
  43.9 7.4 %collective-permute-start.2 = (f32[1,2,128,1,128]{4,3,2,1,0:T(1,128)S(1)}, f32[1,2,128,1,128]{4,3,2,1,0:T(1,128)S(1)}, u32[]{:S(2)}, u32[]{:S(2)}) collective-permute-start(f32[1,2,128,1,128]{4,3,2,1,0:T(1,128)S(1)} %get-tuple-element.69), channel_id=1, source_target_pairs={{0,1},{1,2},{2,3},{4,5},{5,6},{6,7},{8,9},{9,10},{10,11},{12,13},{... | collective-permute-start | bytes 393224 | tf_op jit(solution)/shard_map/ppermute | solution.py:22
  53.9 7.3 %collective-permute-start.5 = (f32[1,2,128,1,128]{4,3,2,1,0:T(1,128)S(1)}, f32[1,2,128,1,128]{4,3,2,1,0:T(1,128)S(1)}, u32[]{:S(2)}, u32[]{:S(2)}) collective-permute-start(f32[1,2,128,1,128]{4,3,2,1,0:T(1,128)S(1)} %get-tuple-element.66), channel_id=1, source_target_pairs={{1,0},{2,1},{3,2},{5,4},{6,5},{7,6},{9,8},{10,9},{11,10},{13,12},{... | collective-permute-start | bytes 393224 | tf_op jit(solution)/shard_map/ppermute | solution.py:23
  55.2 7.5 %collective-permute-start.4 = (f32[1,2,128,1,128]{4,3,2,1,0:T(1,128)S(1)}, f32[1,2,128,1,128]{4,3,2,1,0:T(1,128)S(1)}, u32[]{:S(2)}, u32[]{:S(2)}) collective-permute-start(f32[1,2,128,1,128]{4,3,2,1,0:T(1,128)S(1)} %get-tuple-element.65), channel_id=1, source_target_pairs={{0,1},{1,2},{2,3},{4,5},{5,6},{6,7},{8,9},{9,10},{10,11},{12,13},{... | collective-permute-start | bytes 393224 | tf_op jit(solution)/shard_map/ppermute | solution.py:22
  65.0 7.3 %collective-permute-start.7 = (f32[1,2,128,1,128]{4,3,2,1,0:T(1,128)S(1)}, f32[1,2,128,1,128]{4,3,2,1,0:T(1,128)S(1)}, u32[]{:S(2)}, u32[]{:S(2)}) collective-permute-start(f32[1,2,128,1,128]{4,3,2,1,0:T(1,128)S(1)} %get-tuple-element.62), channel_id=1, source_target_pairs={{1,0},{2,1},{3,2},{5,4},{6,5},{7,6},{9,8},{10,9},{11,10},{13,12},{... | collective-permute-start | bytes 393224 | tf_op jit(solution)/shard_map/ppermute | solution.py:23
  66.3 7.5 %collective-permute-start.6 = (f32[1,2,128,1,128]{4,3,2,1,0:T(1,128)S(1)}, f32[1,2,128,1,128]{4,3,2,1,0:T(1,128)S(1)}, u32[]{:S(2)}, u32[]{:S(2)}) collective-permute-start(f32[1,2,128,1,128]{4,3,2,1,0:T(1,128)S(1)} %get-tuple-element.61), channel_id=1, source_target_pairs={{0,1},{1,2},{2,3},{4,5},{5,6},{6,7},{8,9},{9,10},{10,11},{12,13},{... | collective-permute-start | bytes 393224 | tf_op jit(solution)/shard_map/ppermute | solution.py:22
  77.4 18.3 %collective-permute-start.15 = (f32[1,2,128,1,128]{4,3,2,1,0:T(1,128)S(1)}, f32[1,2,128,1,128]{4,3,2,1,0:T(1,128)S(1)}, u32[]{:S(2)}, u32[]{:S(2)}) collective-permute-start(f32[1,2,128,1,128]{4,3,2,1,0:T(1,128)S(1)} %get-tuple-element.54), channel_id=1, source_target_pairs={{1,0},{2,1},{3,2},{5,4},{6,5},{7,6},{9,8},{10,9},{11,10},{13,12},{... | collective-permute-start | bytes 393224 | tf_op jit(solution)/shard_map/ppermute | solution.py:23
  78.7 17.0 %collective-permute-start.14 = (f32[1,2,128,1,128]{4,3,2,1,0:T(1,128)S(1)}, f32[1,2,128,1,128]{4,3,2,1,0:T(1,128)S(1)}, u32[]{:S(2)}, u32[]{:S(2)}) collective-permute-start(f32[1,2,128,1,128]{4,3,2,1,0:T(1,128)S(1)} %get-tuple-element.53), channel_id=1, source_target_pairs={{0,1},{1,2},{2,3},{4,5},{5,6},{6,7},{8,9},{9,10},{10,11},{12,13},{... | collective-permute-start | bytes 393224 | tf_op jit(solution)/shard_map/ppermute | solution.py:22
  98.8 1.5 copy-start.25
  98.8 1.5 copy-start.44
  100.3 64.2 %all-gather.5.cloned.1.call-start = ((), (), s32[]{:S(2)}) async-start(), calls=%async_computation.3 | async-start | bytes 1769472 | tf_op jit(solution)/shard_map/all_gather | solution.py:145
  100.5 37.4 %copy-start.22 = (f32[3,16,8,128]{3,2,1,0:T(8,128)S(1)}, f32[3,16,8,128]{3,2,1,0:T(8,128)}, u32[]{:S(2)}) copy-start(f32[3,16,8,128]{3,2,1,0:T(8,128)} %param.9) | copy-start | bytes 589828
  100.5 37.4 %copy-start.36 = (f32[3,16,8,128]{3,2,1,0:T(8,128)S(1)}, f32[3,16,8,128]{3,2,1,0:T(8,128)}, u32[]{:S(2)}) copy-start(f32[3,16,8,128]{3,2,1,0:T(8,128)} %param.8) | copy-start | bytes 589828
  101.3 37.4 %copy-start.39 = (f32[1,16,8,128]{3,2,1,0:T(8,128)}, f32[1,16,8,128]{3,2,1,0:T(8,128)S(1)}, u32[]{:S(2)}) copy-start(f32[1,16,8,128]{3,2,1,0:T(8,128)S(1)} %fusion.156) | copy-start | bytes 196612
  101.4 43.9 %copy-start.41 = (f32[1,16,8,128]{3,2,1,0:T(8,128)}, f32[1,16,8,128]{3,2,1,0:T(8,128)S(1)}, u32[]{:S(2)}) copy-start(f32[1,16,8,128]{3,2,1,0:T(8,128)S(1)} %fusion.154) | copy-start | bytes 196612
  138.7 125.3 %reduce-scatter.11.cloned.1.call-start = ((), (), s32[]{:S(2)}) async-start(), calls=%async_computation.5 | async-start | bytes 1769472
  138.9 6.4 %copy-start.15 = (f32[3,16,8,128]{3,2,1,0:T(8,128)S(1)}, f32[3,16,8,128]{3,2,1,0:T(8,128)}, u32[]{:S(2)}) copy-start(f32[3,16,8,128]{3,2,1,0:T(8,128)} %multiply_subtract_fusion.9) | copy-start | bytes 589828
  139.0 10.7 %collective-permute-start.9 = (f32[1,2,128,1,128]{4,3,2,1,0:T(1,128)S(1)}, f32[1,2,128,1,128]{4,3,2,1,0:T(1,128)S(1)}, u32[]{:S(2)}, u32[]{:S(2)}) collective-permute-start(f32[1,2,128,1,128]{4,3,2,1,0:T(1,128)S(1)} %get-tuple-element.58), channel_id=1, source_target_pairs={{1,0},{2,1},{3,2},{5,4},{6,5},{7,6},{9,8},{10,9},{11,10},{13,12},{... | collective-permute-start | bytes 393224 | tf_op jit(solution)/shard_map/ppermute | solution.py:23
  140.4 9.3 %collective-permute-start.8 = (f32[1,2,128,1,128]{4,3,2,1,0:T(1,128)S(1)}, f32[1,2,128,1,128]{4,3,2,1,0:T(1,128)S(1)}, u32[]{:S(2)}, u32[]{:S(2)}) collective-permute-start(f32[1,2,128,1,128]{4,3,2,1,0:T(1,128)S(1)} %get-tuple-element.57), channel_id=1, source_target_pairs={{0,1},{1,2},{2,3},{4,5},{5,6},{6,7},{8,9},{9,10},{10,11},{12,13},{... | collective-permute-start | bytes 393224 | tf_op jit(solution)/shard_map/ppermute | solution.py:22
  145.3 11.9 %copy-start.7 = (f32[1,2,128,8,127]{4,3,2,1,0:T(8,128)}, f32[1,2,128,8,127]{4,3,2,1,0:T(8,128)S(1)}, u32[]{:S(2)}) copy-start(f32[1,2,128,8,127]{4,3,2,1,0:T(8,128)S(1)} %get-tuple-element.55) | copy-start | bytes 3121156
  145.3 11.9 %copy-start.9 = (f32[1,2,128,8,127]{4,3,2,1,0:T(8,128)}, f32[1,2,128,8,127]{4,3,2,1,0:T(8,128)S(1)}, u32[]{:S(2)}) copy-start(f32[1,2,128,8,127]{4,3,2,1,0:T(8,128)S(1)} %get-tuple-element.56) | copy-start | bytes 3121156
  145.3 4.8 %collective-permute-start.23 = (f32[3,1,8,128]{3,2,1,0:T(8,128)S(1)}, f32[3,1,8,128]{3,2,1,0:T(8,128)S(1)}, u32[]{:S(2)}, u32[]{:S(2)}) collective-permute-start(f32[3,1,8,128]{3,2,1,0:T(8,128)S(1)} %get-tuple-element.90), channel_id=1, source_target_pairs={{4,0},{8,4},{12,8},{16,12},{20,16},{24,20},{28,24},{5,1},{9,5},{13... | collective-permute-start | bytes 36872 | tf_op jit(solution)/shard_map/ppermute | solution.py:23
  146.6 3.9 %collective-permute-start.22 = (f32[3,1,8,128]{3,2,1,0:T(8,128)S(1)}, f32[3,1,8,128]{3,2,1,0:T(8,128)S(1)}, u32[]{:S(2)}, u32[]{:S(2)}) collective-permute-start(f32[3,1,8,128]{3,2,1,0:T(8,128)S(1)} %get-tuple-element.89), channel_id=1, source_target_pairs={{0,4},{4,8},{8,12},{12,16},{16,20},{20,24},{24,28},{1,5},{5,9},{9,... | collective-permute-start | bytes 36872 | tf_op jit(solution)/shard_map/ppermute | solution.py:22
  149.7 7.5 %copy-start.28 = (f32[1,2,128,1,128]{4,3,2,1,0:T(1,128)}, f32[1,2,128,1,128]{4,3,2,1,0:T(1,128)S(1)}, u32[]{:S(2)}) copy-start(f32[1,2,128,1,128]{4,3,2,1,0:T(1,128)S(1)} %collective-permute-done.9) | copy-start | bytes 393220
  149.7 7.5 %copy-start.32 = (f32[1,2,128,1,128]{4,3,2,1,0:T(1,128)}, f32[1,2,128,1,128]{4,3,2,1,0:T(1,128)S(1)}, u32[]{:S(2)}) copy-start(f32[1,2,128,1,128]{4,3,2,1,0:T(1,128)S(1)} %collective-permute-done.8) | copy-start | bytes 393220
  150.1 7.1 %copy-start.1 = (f32[1,2,130,10,128]{4,3,2,1,0:T(8,128)}, f32[1,2,130,10,128]{4,3,2,1,0:T(8,128)S(1)}, u32[]{:S(2)}) copy-start(f32[1,2,130,10,128]{4,3,2,1,0:T(8,128)S(1)} %select_maximum_fusion.13) | copy-start | bytes 3993604
  150.5 6.7 %collective-permute-start.25 = (f32[3,18,1,128]{3,2,1,0:T(1,128)S(1)}, f32[3,18,1,128]{3,2,1,0:T(1,128)S(1)}, u32[]{:S(2)}, u32[]{:S(2)}) collective-permute-start(f32[3,18,1,128]{3,2,1,0:T(1,128)S(1)} %get-tuple-element.86), channel_id=1, source_target_pairs={{1,0},{2,1},{3,2},{5,4},{6,5},{7,6},{9,8},{10,9},{11,10},{13,12},{... | collective-permute-start | bytes 82952 | tf_op jit(solution)/shard_map/ppermute | solution.py:23
  151.8 6.1 %collective-permute-start.24 = (f32[3,18,1,128]{3,2,1,0:T(1,128)S(1)}, f32[3,18,1,128]{3,2,1,0:T(1,128)S(1)}, u32[]{:S(2)}, u32[]{:S(2)}) collective-permute-start(f32[3,18,1,128]{3,2,1,0:T(1,128)S(1)} %get-tuple-element.85), channel_id=1, source_target_pairs={{0,1},{1,2},{2,3},{4,5},{5,6},{6,7},{8,9},{9,10},{10,11},{12,13},{... | collective-permute-start | bytes 82952 | tf_op jit(solution)/shard_map/ppermute | solution.py:22
  158.1 1.6 copy-start.16
  164.5 3.4 %copy-start.2 = (f32[1,2,130,10,128]{4,3,2,1,0:T(8,128)S(1)}, f32[1,2,130,10,128]{4,3,2,1,0:T(8,128)}, u32[]{:S(2)}) copy-start(f32[1,2,130,10,128]{4,3,2,1,0:T(8,128)} %copy-done.1) | copy-start | bytes 3993604
  164.5 3.4 %copy-start.8 = (f32[1,2,128,8,127]{4,3,2,1,0:T(8,128)S(1)}, f32[1,2,128,8,127]{4,3,2,1,0:T(8,128)}, u32[]{:S(2)}) copy-start(f32[1,2,128,8,127]{4,3,2,1,0:T(8,128)} %copy-done.7) | copy-start | bytes 3121156
  164.5 3.4 %copy-start.10 = (f32[1,2,128,8,127]{4,3,2,1,0:T(8,128)S(1)}, f32[1,2,128,8,127]{4,3,2,1,0:T(8,128)}, u32[]{:S(2)}) copy-start(f32[1,2,128,8,127]{4,3,2,1,0:T(8,128)} %copy-done.9) | copy-start | bytes 3121156
  164.5 3.4 %copy-start.29 = (f32[1,2,128,1,128]{4,3,2,1,0:T(1,128)S(1)}, f32[1,2,128,1,128]{4,3,2,1,0:T(1,128)}, u32[]{:S(2)}) copy-start(f32[1,2,128,1,128]{4,3,2,1,0:T(1,128)} %copy-done.28) | copy-start | bytes 393220
  164.5 3.4 %copy-start.33 = (f32[1,2,128,1,128]{4,3,2,1,0:T(1,128)S(1)}, f32[1,2,128,1,128]{4,3,2,1,0:T(1,128)}, u32[]{:S(2)}) copy-start(f32[1,2,128,1,128]{4,3,2,1,0:T(1,128)} %copy-done.32) | copy-start | bytes 393220
  169.5 7.5 %collective-permute-start.17 = (f32[1,2,128,1,128]{4,3,2,1,0:T(1,128)S(1)}, f32[1,2,128,1,128]{4,3,2,1,0:T(1,128)S(1)}, u32[]{:S(2)}, u32[]{:S(2)}) collective-permute-start(f32[1,2,128,1,128]{4,3,2,1,0:T(1,128)S(1)} %get-tuple-element.52), channel_id=1, source_target_pairs={{1,0},{2,1},{3,2},{5,4},{6,5},{7,6},{9,8},{10,9},{11,10},{13,12},{... | collective-permute-start | bytes 393224 | tf_op jit(solution)/shard_map/ppermute | solution.py:23
  170.8 7.4 %collective-permute-start.16 = (f32[1,2,128,1,128]{4,3,2,1,0:T(1,128)S(1)}, f32[1,2,128,1,128]{4,3,2,1,0:T(1,128)S(1)}, u32[]{:S(2)}, u32[]{:S(2)}) collective-permute-start(f32[1,2,128,1,128]{4,3,2,1,0:T(1,128)S(1)} %get-tuple-element.51), channel_id=1, source_target_pairs={{0,1},{1,2},{2,3},{4,5},{5,6},{6,7},{8,9},{9,10},{10,11},{12,13},{... | collective-permute-start | bytes 393224 | tf_op jit(solution)/shard_map/ppermute | solution.py:22
  180.8 7.3 %collective-permute-start.19 = (f32[1,2,128,1,128]{4,3,2,1,0:T(1,128)S(1)}, f32[1,2,128,1,128]{4,3,2,1,0:T(1,128)S(1)}, u32[]{:S(2)}, u32[]{:S(2)}) collective-permute-start(f32[1,2,128,1,128]{4,3,2,1,0:T(1,128)S(1)} %get-tuple-element.48), channel_id=1, source_target_pairs={{1,0},{2,1},{3,2},{5,4},{6,5},{7,6},{9,8},{10,9},{11,10},{13,12},{... | collective-permute-start | bytes 393224 | tf_op jit(solution)/shard_map/ppermute | solution.py:23
  182.1 7.5 %collective-permute-start.18 = (f32[1,2,128,1,128]{4,3,2,1,0:T(1,128)S(1)}, f32[1,2,128,1,128]{4,3,2,1,0:T(1,128)S(1)}, u32[]{:S(2)}, u32[]{:S(2)}) collective-permute-start(f32[1,2,128,1,128]{4,3,2,1,0:T(1,128)S(1)} %get-tuple-element.47), channel_id=1, source_target_pairs={{0,1},{1,2},{2,3},{4,5},{5,6},{6,7},{8,9},{9,10},{10,11},{12,13},{... | collective-permute-start | bytes 393224 | tf_op jit(solution)/shard_map/ppermute | solution.py:22
  191.9 7.3 %collective-permute-start.21 = (f32[1,2,128,1,128]{4,3,2,1,0:T(1,128)S(1)}, f32[1,2,128,1,128]{4,3,2,1,0:T(1,128)S(1)}, u32[]{:S(2)}, u32[]{:S(2)}) collective-permute-start(f32[1,2,128,1,128]{4,3,2,1,0:T(1,128)S(1)} %get-tuple-element.44), channel_id=1, source_target_pairs={{1,0},{2,1},{3,2},{5,4},{6,5},{7,6},{9,8},{10,9},{11,10},{13,12},{... | collective-permute-start | bytes 393224 | tf_op jit(solution)/shard_map/ppermute | solution.py:23
  193.2 7.5 %collective-permute-start.20 = (f32[1,2,128,1,128]{4,3,2,1,0:T(1,128)S(1)}, f32[1,2,128,1,128]{4,3,2,1,0:T(1,128)S(1)}, u32[]{:S(2)}, u32[]{:S(2)}) collective-permute-start(f32[1,2,128,1,128]{4,3,2,1,0:T(1,128)S(1)} %get-tuple-element.43), channel_id=1, source_target_pairs={{0,1},{1,2},{2,3},{4,5},{5,6},{6,7},{8,9},{9,10},{10,11},{12,13},{... | collective-permute-start | bytes 393224 | tf_op jit(solution)/shard_map/ppermute | solution.py:22
  203.1 7.5 %copy-start.26 = (f32[17,9,128]{2,1,0:T(8,128)S(1)}, f32[17,9,128]{2,1,0:T(8,128)}, u32[]{:S(2)}) copy-start(f32[17,9,128]{2,1,0:T(8,128)} %fusion.125) | copy-start | bytes 235012
  204.3 19.1 %collective-permute-start.27 = (f32[1,2,128,1,128]{4,3,2,1,0:T(1,128)S(1)}, f32[1,2,128,1,128]{4,3,2,1,0:T(1,128)S(1)}, u32[]{:S(2)}, u32[]{:S(2)}) collective-permute-start(f32[1,2,128,1,128]{4,3,2,1,0:T(1,128)S(1)} %get-tuple-element.40), channel_id=1, source_target_pairs={{1,0},{2,1},{3,2},{5,4},{6,5},{7,6},{9,8},{10,9},{11,10},{13,12},{... | collective-permute-start | bytes 393224 | tf_op jit(solution)/shard_map/ppermute | solution.py:23
  205.6 17.8 %collective-permute-start.26 = (f32[1,2,128,1,128]{4,3,2,1,0:T(1,128)S(1)}, f32[1,2,128,1,128]{4,3,2,1,0:T(1,128)S(1)}, u32[]{:S(2)}, u32[]{:S(2)}) collective-permute-start(f32[1,2,128,1,128]{4,3,2,1,0:T(1,128)S(1)} %get-tuple-element.39), channel_id=1, source_target_pairs={{0,1},{1,2},{2,3},{4,5},{5,6},{6,7},{8,9},{9,10},{10,11},{12,13},{... | collective-permute-start | bytes 393224 | tf_op jit(solution)/shard_map/ppermute | solution.py:22
  226.6 1.5 copy-start.17
  229.0 36.0 %copy-start.24 = (f32[2,8,24,128]{3,2,1,0:T(8,128)S(1)}, f32[2,8,24,128]{3,2,1,0:T(8,128)}, u32[]{:S(2)}) copy-start(f32[2,8,24,128]{3,2,1,0:T(8,128)} %copy-done.23) | copy-start | bytes 589828
  229.1 36.0 %copy-start.37 = (f32[3,16,8,128]{3,2,1,0:T(8,128)S(1)}, f32[3,16,8,128]{3,2,1,0:T(8,128)}, u32[]{:S(2)}) copy-start(f32[3,16,8,128]{3,2,1,0:T(8,128)} %param.8) | copy-start | bytes 589828
  229.1 36.0 %copy-start.40 = (f32[1,16,8,128]{3,2,1,0:T(8,128)S(1)}, f32[1,16,8,128]{3,2,1,0:T(8,128)}, u32[]{:S(2)}) copy-start(f32[1,16,8,128]{3,2,1,0:T(8,128)} %copy-done.39) | copy-start | bytes 196612
  229.1 36.0 %copy-start.42 = (f32[1,16,8,128]{3,2,1,0:T(8,128)S(1)}, f32[1,16,8,128]{3,2,1,0:T(8,128)}, u32[]{:S(2)}) copy-start(f32[1,16,8,128]{3,2,1,0:T(8,128)} %copy-done.41) | copy-start | bytes 196612
  (15 other events, 16.3 us)
Sparse Core Ops, SparseCore 0:
  9.9 28.3 all-gather.2
  100.4 35.8 reduce-scatter.8
  138.9 25.6 all-gather.4
  228.2 35.8 reduce-scatter.10
where the time goes:
time: 274 us; the launch traced here: 272 us
  waiting for transfers between devices  92.7 us (34%)
  starting transfers between devices  81.9 us (30%)
  other arithmetic  36.6 us (13%)
  blocking collectives  22.8 us (8%)
  local copies, waits for them, and re-layouts  21.4 us (8%)
  between operations  17 us (6%)
    unnamed x6, waiting for transfers between devices  69.3 us
    ppermute x14, starting transfers between devices, extended(): before = lax.ppermute(last, axis, up)  63.5 us
    psum x2, blocking collectives, per_device(): norm = lax.psum(local_norm, 'slab')  22.8 us
    ppermute x14, starting transfers between devices, extended(): after = lax.ppermute(leading, axis, down)  18.2 us
    unnamed x102, local copies, waits for them, and re-layouts  11.8 us
    ppermute x14, waiting for transfers between devices, extended(): before = lax.ppermute(last, axis, up)  9.86 us
    sub x8, other arithmetic, hamiltonian(): along_x[0] + along_x[1] + along_y[0] + along_y[1] + along_z[0] + along_z[1]  7.32 us
    ppermute x14, waiting for transfers between devices, extended(): after = lax.ppermute(leading, axis, down)  6.88 us
  transfers between devices with their start and end apart: 32, of which 20 were waited for; matrix products, arithmetic and copies ran while one was open for 6% of the time, Pallas kernels for 0%

commit v1 on v0

v1 whole, which is shorter than its diff:
```python
import functools

import jax
import jax.numpy as jnp
from jax import lax
from jax.experimental import pallas as pl
from jax.experimental.pallas import tpu as pltpu
from jax.sharding import PartitionSpec as P

TERMS = 4
STEPS = 2

time_step = 0.3
wave_step = 0.5
epsilon = 1e-06

MESH = pl.DeviceIdType.MESH
F32 = jnp.float32


def kernel(
    n_orb,
    n_slab,
    orb_ref,
    pot_ref,
    occ_ref,
    e_ref,
    a_ref,
    out_ref,
    eout_ref,
    aout_ref,
    ta,
    tb,
    tot,
    w3,
    af,
    azb,
    sb,
    hz,
    cr,
    hs,
    azs,
    azr,
    enew,
    anew,
    jmine,
    jsend,
    prx,
    jsum,
    rsx,
    nbs,
    nbr,
    ag_s,
    ag_r,
    fw_s,
    fw_r,
    hz_s,
    hz_r,
    az_s,
    az_r,
    pr_s,
    pr_r,
    rs_s,
    rs_r,
    nb_s,
    nb_r,
):
    groups = n_orb // 2
    _, _, nx, zb, ny = orb_ref.shape
    xb = a_ref.shape[1]
    xc = 8 if nx % 8 == 0 and xb % 8 == 0 else xb
    cells = nx * zb * n_slab * ny
    me = lax.axis_index("orb")
    me_s = lax.axis_index("slab")
    me_g = me // 2
    core = me % 2
    partner = me_g * 2 + (1 - core)
    has = (me_s > 0, me_s < n_slab - 1)
    nbr_dev = (me_s - 1, me_s + 1)

    barrier = pltpu.get_barrier_semaphore()

    def greet(o, s):
        pl.semaphore_signal(barrier, inc=1, device_id=(o, s), device_id_type=MESH)

    def group(d):
        return lax.rem(me_g + d, groups)

    def source(d):
        return lax.rem(me_g + groups - d, groups)

    greet(partner, me_s)
    for d in range(1, groups):
        greet(group(d) * 2 + core, me_s)
    for d in range(1, n_slab):
        greet(me, lax.rem(me_s + d, n_slab))

    row = lax.broadcasted_iota(jnp.int32, (1, zb, ny), 1)
    lane = lax.broadcasted_iota(jnp.int32, (1, zb, ny), 2)
    edge = (row == 0, row == zb - 1)
    first_lane, last_lane = lane == 0, lane == ny - 1
    sends = []

    def remote(src, dst, ss, rs, o, s):
        return pltpu.make_async_remote_copy(
            src_ref=src, dst_ref=dst, send_sem=ss, recv_sem=rs, device_id=(o, s), device_id_type=MESH
        )

    def y_next(v):
        return jnp.where(last_lane, 0.0, pltpu.roll(v, ny - 1, 2))

    def y_prev(v):
        return jnp.where(first_lane, 0.0, pltpu.roll(v, 1, 2))

    def z_next(v, halo=0.0):
        return jnp.where(edge[1], halo, pltpu.roll(v, zb - 1, 1))

    def z_prev(v, halo=0.0):
        return jnp.where(edge[0], halo, pltpu.roll(v, 1, 1))

    def halo_copy(h, side):
        return remote(
            sb.at[h, side], hz.at[h, 1 - side], hz_s.at[h, side], hz_r.at[h, 1 - side], me, nbr_dev[side]
        )

    def send_halo(h):
        for side in range(2):

            @pl.when(has[side])
            def _():
                halo_copy(h, side).start()

    def wait_halo(h):
        for side in range(2):

            @pl.when(has[side])
            def _():
                remote(
                    sb.at[h, side], hz.at[h, side], hz_s.at[h, side], hz_r.at[h, side], me, nbr_dev[side]
                ).wait_recv()

    def wait_halo_sent(h):
        for side in range(2):

            @pl.when(has[side])
            def _():
                halo_copy(h, side).wait_send()

    zero_x = jnp.zeros((zb, ny), F32)
    for buf in (ta, tb, tot):
        for part in range(2):
            buf[part, 0] = zero_x
            buf[part, nx + 1] = zero_x
    for step in range(STEPS):
        for comp in range(3):
            af[step, comp, 0] = zero_x
            af[step, comp, nx + 1] = zero_x

    def load_start(i, carry):
        for part in range(2):
            v = orb_ref[0, part, pl.ds(i * xc, xc)]
            ta[part, pl.ds(1 + i * xc, xc)] = v
            tot[part, pl.ds(1 + i * xc, xc)] = v
            sb[0, 0, part, pl.ds(i * xc, xc)] = v[:, 0, :]
            sb[0, 1, part, pl.ds(i * xc, xc)] = v[:, zb - 1, :]
        return carry

    lax.fori_loop(0, nx // xc, load_start, 0)

    for side in range(2):

        @pl.when(jnp.logical_not(has[side]))
        def _():
            for h in range(STEPS * (TERMS + 1)):
                hz[h, side] = jnp.zeros(hz.shape[2:], F32)
            for step in range(STEPS):
                azr[step, side] = jnp.zeros(azr.shape[2:], F32)

    pl.semaphore_wait(barrier, 1 + (groups - 1) + (n_slab - 1))

    def block(o):
        return pl.ds(1 + o * xb, xb)

    def gather_fields(step, src):
        copies = []
        for d in range(1, groups):
            c = remote(src, af.at[step, :, block(me)], ag_s.at[step, d], ag_r.at[step, d], group(d) * 2 + core, me_s)
            c.start()
            sends.append(c)
        c = remote(src, af.at[step, :, block(me)], fw_s.at[step, 0], fw_r.at[step, 0], partner, me_s)
        c.start()
        sends.append(c)

    def weigh(step, o):
        def rows(i, carry):
            x = o * xb + i * xc
            a = [af[step, comp, pl.ds(1 + x, xc)] for comp in range(3)]
            w3[pl.ds(x, xc)] = (
                pot_ref[pl.ds(x, xc)] + 0.5 * (a[0] * a[0] + a[1] * a[1] + a[2] * a[2]) + 3.0
            )
            azb[0, pl.ds(x, xc)] = a[2][:, 0, :]
            azb[1, pl.ds(x, xc)] = a[2][:, zb - 1, :]
            return carry

        lax.fori_loop(0, xb // xc, rows, 0)

    def finish_gather(step, src):
        for comp in range(3):
            af[step, comp, block(me)] = src[comp]
        weigh(step, me)
        for d in range(1, groups):
            o = source(d) * 2 + core
            remote(
                src, af.at[step, :, block(o)], ag_s.at[step, d], ag_r.at[step, d], group(d) * 2 + core, me_s
            ).wait_recv()
            c = remote(
                af.at[step, :, block(o)], af.at[step, :, block(o)], fw_s.at[step, d], fw_r.at[step, d], partner, me_s
            )
            c.start()
            sends.append(c)
            weigh(step, o)
        for d in range(groups):
            o = source(d) * 2 + (1 - core)
            remote(
                af.at[step, :, block(o)], af.at[step, :, block(o)], fw_s.at[step, d], fw_r.at[step, d], partner, me_s
            ).wait_recv()
            weigh(step, o)

    def az_copy(step, side):
        return remote(
            azs.at[step, side],
            azr.at[step, 1 - side],
            az_s.at[step, side],
            az_r.at[step, 1 - side],
            me,
            nbr_dev[side],
        )

    def send_az(step):
        for comp in range(3):
            v = af[step, comp, pl.ds(me * xb, xb + 2)]
            azs[step, 0, comp] = v[:, 0, :]
            azs[step, 1, comp] = v[:, zb - 1, :]
        for side in range(2):

            @pl.when(has[side])
            def _():
                az_copy(step, side).start()

    def half_fields(step, e_src):
        for side in range(2):

            @pl.when(has[side])
            def _():
                remote(
                    azs.at[step, side],
                    azr.at[step, side],
                    az_s.at[step, side],
                    az_r.at[step, side],
                    me,
                    nbr_dev[side],
                ).wait_recv()

        def rows(i, carry):
            x = me * xb + 1 + i

            def at(comp, dx):
                return af[step, comp, pl.ds(x + dx, 1)]

            def up(comp, dx):
                return z_next(at(comp, dx), azr[step, 1, comp, pl.ds(1 + i + dx, 1)][:, None, :])

            def down(comp, dx):
                return z_prev(at(comp, dx), azr[step, 0, comp, pl.ds(1 + i + dx, 1)][:, None, :])

            ax, ay, az = at(0, 0), at(1, 0), at(2, 0)
            ax_m, ay_p, az_p = at(0, -1), at(1, 1), at(2, 1)
            c_x = (
                (ay_p - ay - y_prev(ay_p) + y_prev(ay))
                + (az_p - az - down(2, 1) + down(2, 0))
                - (y_next(ax) + y_prev(ax) + up(0, 0) + down(0, 0) - 4.0 * ax)
            )
            c_y = (
                (y_next(ax) - ax - y_next(ax_m) + ax_m)
                + (y_next(az) - az - y_next(down(2, 0)) + down(2, 0))
                - (ay_p + at(1, -1) + up(1, 0) + down(1, 0) - 4.0 * ay)
            )
            c_z = (
                (up(0, 0) - ax - up(0, -1) + ax_m)
                + (up(1, 0) - ay - y_prev(up(1, 0)) + y_prev(ay))
                - (az_p + at(2, -1) + y_next(az) + y_prev(az) - 4.0 * az)
            )
            for comp, c in enumerate((c_x, c_y, c_z)):
                enew[step, comp, pl.ds(i, 1)] = e_src[comp, pl.ds(i, 1)] + wave_step * c
            return carry

        lax.fori_loop(0, xb, rows, 0)

    def bulk(step, order, t, tn, h):
        f = time_step / order

        def rows(i, carry):
            x = i * xc
            field = [af[step, comp, pl.ds(1 + x, xc)] for comp in range(3)]
            wt = w3[pl.ds(x, xc)]
            mid, total, drift = [], [], []
            for part in range(2):
                v = t[part, pl.ds(1 + x, xc)]
                xp, xm = t[part, pl.ds(2 + x, xc)], t[part, pl.ds(x, xc)]
                yp, ym = y_next(v), y_prev(v)
                zp, zm = z_next(v), z_prev(v)
                mid.append(v)
                total.append((xp + xm) + (yp + ym) + (zp + zm))
                drift.append(field[0] * (xp - xm) + field[1] * (yp - ym) + field[2] * (zp - zm))
            new_p = f * (wt * mid[1]) - (0.5 * f) * (total[1] + drift[0])
            new_q = (0.5 * f) * (total[0] - drift[1]) - f * (wt * mid[0])
            for part, new in enumerate((new_p, new_q)):
                tn[part, pl.ds(1 + x, xc)] = new
                sb[h, 0, part, pl.ds(x, xc)] = new[:, 0, :]
                sb[h, 1, part, pl.ds(x, xc)] = new[:, zb - 1, :]
            return carry

        lax.fori_loop(0, nx // xc, rows, 0)

    def correct(order, h_in, h_out):
        f = time_step / order
        for side in range(2):
            sign = 2.0 * side - 1.0
            hp, hq, az = hz[h_in, side, 0], hz[h_in, side, 1], azb[side]
            dp = (-0.5 * f) * (hq + sign * az * hp)
            dq = (0.5 * f) * (hp - sign * az * hq)
            cr[side, 0] = dp
            cr[side, 1] = dq
            sb[h_out, side, 0] = sb[h_out, side, 0] + dp
            sb[h_out, side, 1] = sb[h_out, side, 1] + dq

    def fix(tn):
        def rows(i, acc):
            x = i * xc
            for part in range(2):
                low = cr[0, part, pl.ds(x, xc)][:, None, :]
                high = cr[1, part, pl.ds(x, xc)][:, None, :]
                v = tn[part, pl.ds(1 + x, xc)] + jnp.where(edge[0], low, jnp.where(edge[1], high, 0.0))
                tn[part, pl.ds(1 + x, xc)] = v
                s = tot[part, pl.ds(1 + x, xc)] + v
                tot[part, pl.ds(1 + x, xc)] = s
                acc = acc + jnp.sum(s * s, axis=0)
            return acc

        return lax.fori_loop(0, nx // xc, rows, jnp.zeros((zb, ny), F32))

    def current(step, o, s2h, dst):
        def rows(i, carry):
            x = o * xb + i * xc
            mids, diffs = [], []
            for part in range(2):
                v = tot[part, pl.ds(1 + x, xc)]
                low = hs[0, part, pl.ds(x, xc)][:, None, :]
                high = hs[1, part, pl.ds(x, xc)][:, None, :]
                mids.append(v)
                diffs.append(
                    (
                        tot[part, pl.ds(2 + x, xc)] - tot[part, pl.ds(x, xc)],
                        y_next(v) - y_prev(v),
                        z_next(v, high) - z_prev(v, low),
                    )
                )
            u, w = mids
            density = 2.0 * (u * u + w * w)
            for comp in range(3):
                a = af[step, comp, pl.ds(1 + x, xc)]
                dst[comp, pl.ds(i * xc, xc)] = s2h * (
                    u * diffs[1][comp] - w * diffs[0][comp] + a * density
                )
            return carry

        lax.fori_loop(0, xb // xc, rows, 0)

    send_halo(0)
    gather_fields(0, a_ref)
    for step in range(STEPS):
        base = step * (TERMS + 1)
        a_src = a_ref if step == 0 else anew.at[0]
        e_src = e_ref if step == 0 else eout_ref
        finish_gather(step, a_src)
        send_az(step)
        t, tn = ta, tb
        for order in range(1, TERMS + 1):
            bulk(step, order, t, tn, base + order)
            if order > 1 or step == 0:
                wait_halo(base + order - 1)
            correct(order, base + order - 1, base + order)
            send_halo(base + order)
            norm_tile = fix(tn)
            if order == 1:
                half_fields(step, e_src)
            t, tn = tn, t
        nbs[step] = norm_tile
        for d in range(1, n_slab):
            c = remote(
                nbs.at[step], nbr.at[step, d], nb_s.at[step, d], nb_r.at[step, d], me, lax.rem(me_s + d, n_slab)
            )
            c.start()
            sends.append(c)
        for d in range(1, n_slab):
            remote(nbs.at[step], nbr.at[step, d], nb_s.at[step, d], nb_r.at[step, d], me, me_s).wait_recv()
            norm_tile = norm_tile + nbr[step, d]
        norm = jnp.sum(jnp.sum(norm_tile, axis=0, keepdims=True), axis=1, keepdims=True)
        scale = jnp.broadcast_to(1.0 / jnp.sqrt(norm / cells + epsilon), (zb, ny))
        s2h = (scale * scale * (0.5 * (occ_ref[0] * (1.0 / n_orb))))[None]
        wait_halo(base + TERMS)
        for side in range(2):
            for part in range(2):
                total = hz[base, side, part]
                for k in range(1, TERMS + 1):
                    total = total + hz[base + k, side, part]
                hs[side, part] = total
        order_d = list(range(1, groups)) + [0]
        for d in order_d:
            current(step, group(d) * 2 + (1 - core), s2h, jsend.at[step, d])
            c = remote(
                jsend.at[step, d], prx.at[step, d], pr_s.at[step, d], pr_r.at[step, d], partner, me_s
            )
            c.start()
            sends.append(c)
        for d in order_d:
            current(step, group(d) * 2 + core, s2h, jmine.at[d])
            remote(
                jsend.at[step, d], prx.at[step, d], pr_s.at[step, d], pr_r.at[step, d], partner, me_s
            ).wait_recv()
            for comp in range(3):
                jsum[step, d, comp] = jmine[d, comp] + prx[step, d, comp]
            if d:
                c = remote(
                    jsum.at[step, d], rsx.at[step, d], rs_s.at[step, d], rs_r.at[step, d], group(d) * 2 + core, me_s
                )
                c.start()
                sends.append(c)

        def rescale(i, carry):
            x = i * xc
            for part in range(2):
                v = scale[None] * tot[part, pl.ds(1 + x, xc)]
                if step == STEPS - 1:
                    out_ref[0, part, pl.ds(x, xc)] = v
                else:
                    t[part, pl.ds(1 + x, xc)] = v
                    tot[part, pl.ds(1 + x, xc)] = v
            return carry

        lax.fori_loop(0, nx // xc, rescale, 0)
        if step < STEPS - 1:
            for side in range(2):
                for part in range(2):
                    hz[base + TERMS + 1, side, part] = scale[0:1] * hs[side, part]
        for d in range(1, groups):
            remote(
                jsum.at[step, d], rsx.at[step, d], rs_s.at[step, d], rs_r.at[step, d], partner, me_s
            ).wait_recv()

        for comp in range(3):
            flow = jsum[step, 0, comp]
            for d in range(1, groups):
                flow = flow + rsx[step, d, comp]
            e = enew[step, comp] - wave_step * flow
            eout_ref[comp] = e
            a = a_src[comp] - wave_step * e
            if step == STEPS - 1:
                aout_ref[comp] = a
            else:
                anew[step, comp] = a
        if step < STEPS - 1:
            gather_fields(step + 1, anew.at[step])

    for c in sends:
        c.wait_send()
    for h in range(STEPS * (TERMS + 1)):
        if h != TERMS + 1:
            wait_halo_sent(h)
    for step in range(STEPS):
        for side in range(2):

            @pl.when(has[side])
            def _():
                az_copy(step, side).wait_send()


def per_device(orbitals, potential, occupation, e_field, a_field):
    n_orb, n_slab = lax.axis_size("orb"), lax.axis_size("slab")
    _, _, nx, zb, ny = orbitals.shape
    xb = a_field.shape[1]
    groups = n_orb // 2
    halos = STEPS * (TERMS + 1)
    vmem = pl.BlockSpec(memory_space=pltpu.VMEM)

    def sem(*shape):
        return pltpu.SemaphoreType.DMA(shape)

    def buf(*shape):
        return pltpu.VMEM(shape, F32)

    return pl.pallas_call(
        functools.partial(kernel, n_orb, n_slab),
        out_shape=(
            jax.ShapeDtypeStruct(orbitals.shape, F32),
            jax.ShapeDtypeStruct(e_field.shape, F32),
            jax.ShapeDtypeStruct(a_field.shape, F32),
        ),
        in_specs=[vmem, vmem, pl.BlockSpec(memory_space=pltpu.SMEM), vmem, vmem],
        out_specs=(vmem, vmem, vmem),
        scratch_shapes=[
            buf(2, nx + 2, zb, ny),
            buf(2, nx + 2, zb, ny),
            buf(2, nx + 2, zb, ny),
            buf(nx, zb, ny),
            buf(STEPS, 3, nx + 2, zb, ny),
            buf(2, nx, ny),
            buf(halos, 2, 2, nx, ny),
            buf(halos, 2, 2, nx, ny),
            buf(2, 2, nx, ny),
            buf(2, 2, nx, ny),
            buf(STEPS, 2, 3, xb + 2, ny),
            buf(STEPS, 2, 3, xb + 2, ny),
            buf(STEPS, 3, xb, zb, ny),
            buf(STEPS, 3, xb, zb, ny),
            buf(groups, 3, xb, zb, ny),
            buf(STEPS, groups, 3, xb, zb, ny),
            buf(STEPS, groups, 3, xb, zb, ny),
            buf(STEPS, groups, 3, xb, zb, ny),
            buf(STEPS, groups, 3, xb, zb, ny),
            buf(STEPS, zb, ny),
            buf(STEPS, n_slab, zb, ny),
            sem(STEPS, groups),
            sem(STEPS, groups),
            sem(STEPS, groups),
            sem(STEPS, groups),
            sem(halos, 2),
            sem(halos, 2),
            sem(STEPS, 2),
            sem(STEPS, 2),
            sem(STEPS, groups),
            sem(STEPS, groups),
            sem(STEPS, groups),
            sem(STEPS, groups),
            sem(STEPS, n_slab),
            sem(STEPS, n_slab),
        ],
        compiler_params=pltpu.CompilerParams(
            collective_id=0, has_side_effects=True, vmem_limit_bytes=60 * 1024 * 1024
        ),
    )(orbitals, potential, occupation, e_field, a_field)


def solution(mesh):
    return jax.shard_map(
        per_device,
        mesh=mesh,
        in_specs=(
            P("orb", None, None, "slab", None),
            P(None, "slab", None),
            P("orb"),
            P(None, "orb", "slab", None),
            P(None, "orb", "slab", None),
        ),
        out_specs=(
            P("orb", None, None, "slab", None),
            P(None, "orb", "slab", None),
            P(None, "orb", "slab", None),
        ),
        check_vma=False,
    )
```

time: 274 us -> 104 us (0.38)
  Pallas kernels: 0 us -> 98.2 us
  waiting for transfers between devices: 92.7 us -> 0 us
  starting transfers between devices: 81.9 us -> 0 us
  other arithmetic: 36.6 us -> 0 us
  blocking collectives: 22.8 us -> 0 us
  local copies, waits for them, and re-layouts: 21.4 us -> 3.98 us
  between operations: 17 us -> 1.3 us
    pallas_call x0 -> x1, Pallas kernels: none -> 98.2 us  [per_device(): pl.pallas_call(functools.partial(kernel, n_orb, n_slab), out_shape=(jax.S...]
    ppermute x28 -> x0, starting transfers between devices: 81.7 us -> none  [the longest x14 63.5 us: extended(): before = lax.ppermute(last, axis, up)]
    unnamed x6 -> x0, waiting for transfers between devices: 69.3 us -> none
    psum x2 -> x0, blocking collectives: 22.8 us -> none  [per_device(): norm = lax.psum(local_norm, 'slab')]
    ppermute x28 -> x0, waiting for transfers between devices: 16.7 us -> none  [the longest x14 9.86 us: extended(): before = lax.ppermute(last, axis, up)]
    sub x17 -> x0, other arithmetic: 12.4 us -> none  [the longest x8 7.32 us: hamiltonian(): along_x[0] + along_x[1] + along_y[0] + along_y[1] + along_z[0] + along_z[1]]
    mul x18 -> x0, other arithmetic: 11.6 us -> none  [the longest x8 6.8 us: hamiltonian(): 0.5 * (field[0] * (along_x[0] - along_x[1]) + field[1] * (along_y[0] - al...]
    unnamed x102 -> x7, local copies, waits for them, and re-layouts: 11.8 us -> 3.98 us
  transfers between devices with their start and end apart: 32 -> 0, of which waited for: 20 -> 0; matrix products, arithmetic and copies ran while one was open for 6% -> 0% of each run, Pallas kernels for 0% -> 0%
where the time goes in v1:
time: 104 us
  Pallas kernels  98.2 us (94%)
  local copies, waits for them, and re-layouts  3.98 us (4%)
  between operations  1.3 us (1%)
    pallas_call x1, Pallas kernels, per_device(): pl.pallas_call(functools.partial(kernel, n_orb, n_slab), out_shape=(jax.S...  98.2 us
    unnamed x7, local copies, waits for them, and re-layouts  3.98 us

profile of v1, /device:TPU:0, one launch (start us, length us, event | category | flops | bytes accessed | tf_op | source)
XLA Modules:
  0.0 103.5 jit_solution(18323162511042294774)
XLA Ops:
  1.3 98.2 %shard_map.76 = (f32[1,2,128,8,128]{4,3,2,1,0:T(8,128)}, f32[3,16,8,128]{3,2,1,0:T(8,128)}, f32[3,16,8,128]{3,2,1,0:T(8,128)}) custom-call(f32[1,2,128,8,128]{4,3,2,1,0:T(8,128)} %orb_ref.1, f32[128,8,128]{2,1,0:T(8,128)} %pot_ref.1, f32[1]{0:T(128)S(6)} %copy.11.occ_ref, f32[3,16,8,128]{3,2,1,0:T(8,128)} %e_ref.1, f32[3,16,8,128]{3,2,1,0:T(8,128)} %a_ref.1), custom_call_target="tpu_custom_call" | custom-call | tf_op jit(solution)/shard_map/pallas_call | solution.py:502
  99.5 0.0 copy-start.1
  99.5 2.3 %copy.12 = f32[1,2,128,8,128]{4,3,2,1,0:T(8,128)} copy(f32[1,2,128,8,128]{4,3,2,1,0:T(8,128)} %get-tuple-element.6) | data formatting | bytes 2097152
  101.8 0.0 copy-done.1
  101.8 0.0 copy-start
  101.8 0.7 copy.13
  102.5 0.3 copy-done
  102.8 0.7 copy.14
Async XLA Ops:
  99.5 2.3 %copy-start.1 = (f32[3,16,8,128]{3,2,1,0:T(8,128)S(1)}, f32[3,16,8,128]{3,2,1,0:T(8,128)}, u32[]{:S(2)}) copy-start(f32[3,16,8,128]{3,2,1,0:T(8,128)} %get-tuple-element.7) | copy-start | bytes 589828
  101.8 1.0 copy-start

commit v2 on v1

--- a/solution.py
+++ b/solution.py
@@ -27,21 +27,22 @@
     e_ref,
     a_ref,
     out_ref,
-    eout_ref,
-    aout_ref,
+    scale_ref,
+    half_ref,
+    flow_ref,
+    aold_ref,
     ta,
     tb,
     tot,
     w3,
     af,
-    azb,
     sb,
     hz,
-    cr,
     hs,
     azs,
     azr,
     enew,
+    ekeep,
     anew,
     jmine,
     jsend,
@@ -118,33 +119,46 @@
     def z_prev(v, halo=0.0):
         return jnp.where(edge[0], halo, pltpu.roll(v, 1, 1))
 
-    def halo_copy(h, side):
+    def rows_of(o):
+        return pl.ds(o * xb, xb)
+
+    def halo_copy(h, side, o):
         return remote(
-            sb.at[h, side], hz.at[h, 1 - side], hz_s.at[h, side], hz_r.at[h, 1 - side], me, nbr_dev[side]
+            sb.at[h, side, :, rows_of(o)],
+            hz.at[h, 1 - side, :, rows_of(o)],
+            hz_s.at[h, side, o],
+            hz_r.at[h, 1 - side, o],
+            me,
+            nbr_dev[side],
         )
 
-    def send_halo(h):
+    def send_halo(h, o):
         for side in range(2):
 
             @pl.when(has[side])
             def _():
-                halo_copy(h, side).start()
-
-    def wait_halo(h):
+                halo_copy(h, side, o).start()
+
+    def wait_halo(h, o):
         for side in range(2):
 
             @pl.when(has[side])
             def _():
                 remote(
-                    sb.at[h, side], hz.at[h, side], hz_s.at[h, side], hz_r.at[h, side], me, nbr_dev[side]
+                    sb.at[h, side, :, rows_of(o)],
+                    hz.at[h, side, :, rows_of(o)],
+                    hz_s.at[h, side, o],
+                    hz_r.at[h, side, o],
+                    me,
+                    nbr_dev[side],
                 ).wait_recv()
 
-    def wait_halo_sent(h):
+    def wait_halo_sent(h, o):
         for side in range(2):
 
             @pl.when(has[side])
             def _():
-                halo_copy(h, side).wait_send()
+                halo_copy(h, side, o).wait_send()
 
     zero_x = jnp.zeros((zb, ny), F32)
     for buf in (ta, tb, tot):
@@ -156,16 +170,16 @@
             af[step, comp, 0] = zero_x
             af[step, comp, nx + 1] = zero_x
 
-    def load_start(i, carry):
-        for part in range(2):
-            v = orb_ref[0, part, pl.ds(i * xc, xc)]
-            ta[part, pl.ds(1 + i * xc, xc)] = v
-            tot[part, pl.ds(1 + i * xc, xc)] = v
-            sb[0, 0, part, pl.ds(i * xc, xc)] = v[:, 0, :]
-            sb[0, 1, part, pl.ds(i * xc, xc)] = v[:, zb - 1, :]
+    def load_start(o, carry):
+        for i in range(xb // xc):
+            x = o * xb + i * xc
+            for part in range(2):
+                v = orb_ref[0, part, pl.ds(x, xc)]
+                ta[part, pl.ds(1 + x, xc)] = v
+                sb[0, 0, part, pl.ds(x, xc)] = v[:, 0, :]
+                sb[0, 1, part, pl.ds(x, xc)] = v[:, zb - 1, :]
+        send_halo(0, o)
         return carry
-
-    lax.fori_loop(0, nx // xc, load_start, 0)
 
     for side in range(2):
 
@@ -198,16 +212,15 @@
             w3[pl.ds(x, xc)] = (
                 pot_ref[pl.ds(x, xc)] + 0.5 * (a[0] * a[0] + a[1] * a[1] + a[2] * a[2]) + 3.0
             )
-            azb[0, pl.ds(x, xc)] = a[2][:, 0, :]
-            azb[1, pl.ds(x, xc)] = a[2][:, zb - 1, :]
             return carry
 
         lax.fori_loop(0, xb // xc, rows, 0)
 
-    def finish_gather(step, src):
+    def finish_gather(step, src, use):
         for comp in range(3):
             af[step, comp, block(me)] = src[comp]
         weigh(step, me)
+        use(me)
         for d in range(1, groups):
             o = source(d) * 2 + core
             remote(
@@ -219,12 +232,14 @@
             c.start()
             sends.append(c)
             weigh(step, o)
+            use(o)
         for d in range(groups):
             o = source(d) * 2 + (1 - core)
             remote(
                 af.at[step, :, block(o)], af.at[step, :, block(o)], fw_s.at[step, d], fw_r.at[step, d], partner, me_s
             ).wait_recv()
             weigh(step, o)
+            use(o)
 
     def az_copy(step, side):
         return remote(
@@ -296,11 +311,15 @@
 
         lax.fori_loop(0, xb, rows, 0)
 
-    def bulk(step, order, t, tn, h):
+    def term_block(step, order, t, tn, o, acc):
         f = time_step / order
-
-        def rows(i, carry):
-            x = i * xc
+        base = step * (TERMS + 1)
+        h_in, h_out = base + order - 1, base + order
+        if h_in != TERMS + 1:
+            wait_halo(h_in, o)
+
+        def rows(i, acc):
+            x = o * xb + i * xc
             field = [af[step, comp, pl.ds(1 + x, xc)] for comp in range(3)]
             wt = w3[pl.ds(x, xc)]
             mid, total, drift = [], [], []
@@ -308,48 +327,41 @@
                 v = t[part, pl.ds(1 + x, xc)]
                 xp, xm = t[part, pl.ds(2 + x, xc)], t[part, pl.ds(x, xc)]
                 yp, ym = y_next(v), y_prev(v)
-                zp, zm = z_next(v), z_prev(v)
+                zp = z_next(v, hz[h_in, 1, part, pl.ds(x, xc)][:, None, :])
+                zm = z_prev(v, hz[h_in, 0, part, pl.ds(x, xc)][:, None, :])
                 mid.append(v)
                 total.append((xp + xm) + (yp + ym) + (zp + zm))
                 drift.append(field[0] * (xp - xm) + field[1] * (yp - ym) + field[2] * (zp - zm))
             new_p = f * (wt * mid[1]) - (0.5 * f) * (total[1] + drift[0])
             new_q = (0.5 * f) * (total[0] - drift[1]) - f * (wt * mid[0])
             for part, new in enumerate((new_p, new_q)):
-                tn[part, pl.ds(1 + x, xc)] = new
-                sb[h, 0, part, pl.ds(x, xc)] = new[:, 0, :]
-                sb[h, 1, part, pl.ds(x, xc)] = new[:, zb - 1, :]
-            return carry
-
-        lax.fori_loop(0, nx // xc, rows, 0)
-
-    def correct(order, h_in, h_out):
-        f = time_step / order
-        for side in range(2):
-            sign = 2.0 * side - 1.0
-            hp, hq, az = hz[h_in, side, 0], hz[h_in, side, 1], azb[side]
-            dp = (-0.5 * f) * (hq + sign * az * hp)
-            dq = (0.5 * f) * (hp - sign * az * hq)
-            cr[side, 0] = dp
-            cr[side, 1] = dq
-            sb[h_out, side, 0] = sb[h_out, side, 0] + dp
-            sb[h_out, side, 1] = sb[h_out, side, 1] + dq
-
-    def fix(tn):
-        def rows(i, acc):
-            x = i * xc
+                sb[h_out, 0, part, pl.ds(x, xc)] = new[:, 0, :]
+                sb[h_out, 1, part, pl.ds(x, xc)] = new[:, zb - 1, :]
+                if order == 1:
+                    s = mid[part] + new
+                else:
+                    s = tot[part, pl.ds(1 + x, xc)] + new
+                tot[part, pl.ds(1 + x, xc)] = s
+                if order < TERMS:
+                    tn[part, pl.ds(1 + x, xc)] = new
+                else:
+                    acc = acc + jnp.sum(s * s, axis=0)
+            return acc
+
+        acc = lax.fori_loop(0, xb // xc, rows, acc)
+        send_halo(h_out, o)
+        return acc
+
+    def current(step, o, s2h, dst):
+        base = step * (TERMS + 1)
+        wait_halo(base + TERMS, o)
+        for side in range(2):
             for part in range(2):
-                low = cr[0, part, pl.ds(x, xc)][:, None, :]
-                high = cr[1, part, pl.ds(x, xc)][:, None, :]
-                v = tn[part, pl.ds(1 + x, xc)] + jnp.where(edge[0], low, jnp.where(edge[1], high, 0.0))
-                tn[part, pl.ds(1 + x, xc)] = v
-                s = tot[part, pl.ds(1 + x, xc)] + v
-                tot[part, pl.ds(1 + x, xc)] = s
-                acc = acc + jnp.sum(s * s, axis=0)
-            return acc
-
-        return lax.fori_loop(0, nx // xc, rows, jnp.zeros((zb, ny), F32))
-
-    def current(step, o, s2h, dst):
+                total = hz[base, side, part, rows_of(o)]
+                for k in range(1, TERMS + 1):
+                    total = total + hz[base + k, side, part, rows_of(o)]
+                hs[side, part, rows_of(o)] = total
+
         def rows(i, carry):
             x = o * xb + i * xc
             mids, diffs = [], []
@@ -369,32 +381,35 @@
             density = 2.0 * (u * u + w * w)
             for comp in range(3):
                 a = af[step, comp, pl.ds(1 + x, xc)]
-                dst[comp, pl.ds(i * xc, xc)] = s2h * (
-                    u * diffs[1][comp] - w * diffs[0][comp] + a * density
-                )
+                j = u * diffs[1][comp] - w * diffs[0][comp] + a * density
+                dst[comp, pl.ds(i * xc, xc)] = j if s2h is None else s2h * j
             return carry
 
         lax.fori_loop(0, xb // xc, rows, 0)
 
-    send_halo(0)
+    none = jnp.zeros((zb, ny), F32)
+    order_d = list(range(1, groups)) + [0]
     gather_fields(0, a_ref)
+    lax.fori_loop(0, n_orb, load_start, 0)
     for step in range(STEPS):
         base = step * (TERMS + 1)
-        a_src = a_ref if step == 0 else anew.at[0]
-        e_src = e_ref if step == 0 else eout_ref
-        finish_gather(step, a_src)
+        a_src = a_ref if step == 0 else anew.at[step - 1]
+        e_src = e_ref if step == 0 else ekeep
+        finish_gather(step, a_src, lambda o: term_block(step, 1, ta, tb, o, none))
         send_az(step)
-        t, tn = ta, tb
-        for order in range(1, TERMS + 1):
-            bulk(step, order, t, tn, base + order)
-            if order > 1 or step == 0:
-                wait_halo(base + order - 1)
-            correct(order, base + order - 1, base + order)
-            send_halo(base + order)
-            norm_tile = fix(tn)
-            if order == 1:
-                half_fields(step, e_src)
+        t, tn = tb, ta
+        for order in range(2, TERMS):
+            lax.fori_loop(
+                0, n_orb, lambda o, acc: term_block(step, order, t, tn, o, acc), none
+            )
             t, tn = tn, t
+
+        def last(j, acc):
+            side, d = j // groups, lax.rem(j % groups + 1, groups)
+            other = side + core - 2 * side * core
+            return term_block(step, TERMS, t, tn, group(d) * 2 + 1 - other, acc)
+
+        norm_tile = lax.fori_loop(0, n_orb, last, none)
         nbs[step] = norm_tile
         for d in range(1, n_slab):
             c = remote(
@@ -402,22 +417,17 @@
             )
             c.start()
             sends.append(c)
+        for d in order_d:
+            current(step, group(d) * 2 + (1 - core), None, jmine.at[d])
         for d in range(1, n_slab):
             remote(nbs.at[step], nbr.at[step, d], nb_s.at[step, d], nb_r.at[step, d], me, me_s).wait_recv()
             norm_tile = norm_tile + nbr[step, d]
         norm = jnp.sum(jnp.sum(norm_tile, axis=0, keepdims=True), axis=1, keepdims=True)
         scale = jnp.broadcast_to(1.0 / jnp.sqrt(norm / cells + epsilon), (zb, ny))
         s2h = (scale * scale * (0.5 * (occ_ref[0] * (1.0 / n_orb))))[None]
-        wait_halo(base + TERMS)
-        for side in range(2):
-            for part in range(2):
-                total = hz[base, side, part]
-                for k in range(1, TERMS + 1):
-                    total = total + hz[base + k, side, part]
-                hs[side, part] = total
-        order_d = list(range(1, groups)) + [0]
         for d in order_d:
-            current(step, group(d) * 2 + (1 - core), s2h, jsend.at[step, d])
+            for comp in range(3):
+                jsend[step, d, comp] = s2h * jmine[d, comp]
             c = remote(
                 jsend.at[step, d], prx.at[step, d], pr_s.at[step, d], pr_r.at[step, d], partner, me_s
             )
@@ -440,15 +450,15 @@
         def rescale(i, carry):
             x = i * xc
             for part in range(2):
-                v = scale[None] * tot[part, pl.ds(1 + x, xc)]
+                v = tot[part, pl.ds(1 + x, xc)]
                 if step == STEPS - 1:
                     out_ref[0, part, pl.ds(x, xc)] = v
                 else:
-                    t[part, pl.ds(1 + x, xc)] = v
-                    tot[part, pl.ds(1 + x, xc)] = v
+                    ta[part, pl.ds(1 + x, xc)] = scale[None] * v
             return carry
 
         lax.fori_loop(0, nx // xc, rescale, 0)
+        half_fields(step, e_src)
         if step < STEPS - 1:
             for side in range(2):
                 for part in range(2):
@@ -462,21 +472,24 @@
             flow = jsum[step, 0, comp]
             for d in range(1, groups):
                 flow = flow + rsx[step, d, comp]
-            e = enew[step, comp] - wave_step * flow
-            eout_ref[comp] = e
-            a = a_src[comp] - wave_step * e
             if step == STEPS - 1:
-                aout_ref[comp] = a
+                half_ref[comp] = enew[step, comp]
+                flow_ref[comp] = flow
+                aold_ref[comp] = a_src[comp]
             else:
-                anew[step, comp] = a
+                e = enew[step, comp] - wave_step * flow
+                ekeep[comp] = e
+                anew[step, comp] = a_src[comp] - wave_step * e
         if step < STEPS - 1:
             gather_fields(step + 1, anew.at[step])
+        else:
+            scale_ref[...] = scale
 
     for c in sends:
         c.wait_send()
     for h in range(STEPS * (TERMS + 1)):
         if h != TERMS + 1:
-            wait_halo_sent(h)
+            lax.fori_loop(0, n_orb, lambda o, carry: (wait_halo_sent(h, o), carry)[1], 0)
     for step in range(STEPS):
         for side in range(2):
 
@@ -499,29 +512,30 @@
     def buf(*shape):
         return pltpu.VMEM(shape, F32)
 
-    return pl.pallas_call(
+    moved, scale, half, flow, a_old = pl.pallas_call(
         functools.partial(kernel, n_orb, n_slab),
         out_shape=(
             jax.ShapeDtypeStruct(orbitals.shape, F32),
+            jax.ShapeDtypeStruct((zb, ny), F32),
             jax.ShapeDtypeStruct(e_field.shape, F32),
-            jax.ShapeDtypeStruct(a_field.shape, F32),
+            jax.ShapeDtypeStruct(e_field.shape, F32),
+            jax.ShapeDtypeStruct(e_field.shape, F32),
         ),
         in_specs=[vmem, vmem, pl.BlockSpec(memory_space=pltpu.SMEM), vmem, vmem],
-        out_specs=(vmem, vmem, vmem),
+        out_specs=(vmem,) * 5,
         scratch_shapes=[
             buf(2, nx + 2, zb, ny),
             buf(2, nx + 2, zb, ny),
             buf(2, nx + 2, zb, ny),
             buf(nx, zb, ny),
             buf(STEPS, 3, nx + 2, zb, ny),
-            buf(2, nx, ny),
             buf(halos, 2, 2, nx, ny),
             buf(halos, 2, 2, nx, ny),
-            buf(2, 2, nx, ny),
             buf(2, 2, nx, ny),
             buf(STEPS, 2, 3, xb + 2, ny),
             buf(STEPS, 2, 3, xb + 2, ny),
             buf(STEPS, 3, xb, zb, ny),
+            buf(3, xb, zb, ny),
             buf(STEPS, 3, xb, zb, ny),
             buf(groups, 3, xb, zb, ny),
             buf(STEPS, groups, 3, xb, zb, ny),
@@ -534,8 +548,8 @@
             sem(STEPS, groups),
             sem(STEPS, groups),
             sem(STEPS, groups),
-            sem(halos, 2),
-            sem(halos, 2),
+            sem(halos, 2, n_orb),
+            sem(halos, 2, n_orb),
             sem(STEPS, 2),
             sem(STEPS, 2),
             sem(STEPS, groups),
@@ -549,6 +563,8 @@
             collective_id=0, has_side_effects=True, vmem_limit_bytes=60 * 1024 * 1024
         ),
     )(orbitals, potential, occupation, e_field, a_field)
+    e_next = half - wave_step * flow
+    return (moved * scale, e_next, a_old - wave_step * e_next)
 
 
 def solution(mesh):

time: 104 us -> 98.8 us (0.950)
  Pallas kernels: 98.2 us -> 92.4 us
  other arithmetic: 0 us -> 4.16 us
  local copies, waits for them, and re-layouts: 3.98 us -> 0.68 us
    pallas_call x1, Pallas kernels: 98.2 us -> 92.4 us  [per_device(): pl.pallas_call(functools.partial(kernel, n_orb, n_slab), out_shape=(jax.S...]
    unnamed x7 -> x2, local copies, waits for them, and re-layouts: 3.98 us -> 0.68 us
    mul x0 -> x1, other arithmetic: none -> 2.26 us  [per_device(): return (moved * scale, e_next, a_old - wave_step * e_next)]
    sub x0 -> x1, other arithmetic: none -> 1.89 us  [per_device(): return (moved * scale, e_next, a_old - wave_step * e_next)]
where the time goes in v2:
time: 98.8 us; the launch traced here: 98.5 us
  Pallas kernels  92.4 us (94%)
  other arithmetic  4.16 us (4%)
  between operations  1.29 us (1%)
    pallas_call x1, Pallas kernels, per_device(): pl.pallas_call(functools.partial(kernel, n_orb, n_slab), out_shape=(jax.S...  92.4 us
    mul x1, other arithmetic, per_device(): return (moved * scale, e_next, a_old - wave_step * e_next)  2.26 us

profile of v2, /device:TPU:0, one launch (start us, length us, event | category | flops | bytes accessed | tf_op | source)
XLA Modules:
  0.0 98.5 jit_solution(15600972401048113915)
XLA Ops:
  1.3 92.4 %shard_map.76 = (f32[1,2,128,8,128]{4,3,2,1,0:T(8,128)}, f32[8,128]{1,0:T(8,128)}, f32[3,16,8,128]{3,2,1,0:T(8,128)}, f32[3,16,8,128]{3,2,1,0:T(8,128)}, f32[3,16,8,128]{3,2,1,0:T(8,128)}) custom-call(f32[1,2,128,8,128]{4,3,2,1,0:T(8,128)} %orb_ref.1, f32[128,8,128]{2,1,0:T(8,128)} %pot_ref.1, f32[1]{0:T(128)S(6)} %copy.8.occ_ref, f32[3,16,8,128]{3,2,1,0:T(8,128)} %e_ref.1, ...), custom_call_target="tpu_custom_call" | custom-call | tf_op jit(solution)/shard_map/pallas_call | solution.py:515
  93.7 1.9 %multiply_subtract_fusion = (f32[3,16,8,128]{3,2,1,0:T(8,128)}, f32[3,16,8,128]{3,2,1,0:T(8,128)}) fusion(f32[3,16,8,128]{3,2,1,0:T(8,128)} %get-tuple-element.12, f32[3,16,8,128]{3,2,1,0:T(8,128)} %get-tuple-element.10, f32[3,16,8,128]{3,2,1,0:T(8,128)} %get-tuple-element.11), kind=kLoop, calls=%fused_computation.1 | loop fusion | flops 196608 | bytes 983040 | tf_op jit(solution)/shard_map/sub | solution.py:567
  95.6 0.0 copy-start
  95.6 0.7 copy-done
  96.3 2.3 %broadcast_multiply_fusion = f32[1,2,128,8,128]{4,3,2,1,0:T(8,128)} fusion(f32[1,2,128,8,128]{4,3,2,1,0:T(8,128)} %get-tuple-element.8, f32[8,128]{1,0:T(8,128)S(1)} %copy-done), kind=kLoop, calls=%fused_computation | loop fusion | flops 262144 | bytes 2101248 | tf_op jit(solution)/shard_map/mul | solution.py:567
Async XLA Ops:
  95.6 0.7 copy-start

commit v3 on v2

--- a/solution.py
+++ b/solution.py
@@ -84,10 +84,23 @@
     def greet(o, s):
         pl.semaphore_signal(barrier, inc=1, device_id=(o, s), device_id_type=MESH)
 
-    def group(d):
-        return lax.rem(me_g + d, groups)
-
-    def source(d):
+    relay = groups == 4
+
+    def group(d, c=None):
+        c = core if c is None else c
+        if not relay:
+            return lax.rem(me_g + d, groups)
+        by_x, by_y = me_g + 1 - 2 * (me_g % 2), lax.rem(me_g + 2, 4)
+        return (
+            me_g,
+            by_x * (1 - c) + by_y * c,
+            by_y * (1 - c) + by_x * c,
+            3 - me_g,
+        )[d]
+
+    def source(d, c=None):
+        if relay:
+            return group(d, c)
         return lax.rem(me_g + groups - d, groups)
 
     greet(partner, me_s)
@@ -196,8 +209,7 @@
         return pl.ds(1 + o * xb, xb)
 
     def gather_fields(step, src):
-        copies = []
-        for d in range(1, groups):
+        for d in range(1, 3 if relay else groups):
             c = remote(src, af.at[step, :, block(me)], ag_s.at[step, d], ag_r.at[step, d], group(d) * 2 + core, me_s)
             c.start()
             sends.append(c)
@@ -221,11 +233,22 @@
             af[step, comp, block(me)] = src[comp]
         weigh(step, me)
         use(me)
-        for d in range(1, groups):
+        for d in (2, 1, 3) if relay else range(1, groups):
             o = source(d) * 2 + core
             remote(
                 src, af.at[step, :, block(o)], ag_s.at[step, d], ag_r.at[step, d], group(d) * 2 + core, me_s
             ).wait_recv()
+            if relay and d == 2:
+                c = remote(
+                    af.at[step, :, block(o)],
+                    af.at[step, :, block(o)],
+                    ag_s.at[step, 3],
+                    ag_r.at[step, 3],
+                    group(1) * 2 + core,
+                    me_s,
+                )
+                c.start()
+                sends.append(c)
             c = remote(
                 af.at[step, :, block(o)], af.at[step, :, block(o)], fw_s.at[step, d], fw_r.at[step, d], partner, me_s
             )
@@ -233,8 +256,8 @@
             sends.append(c)
             weigh(step, o)
             use(o)
-        for d in range(groups):
-            o = source(d) * 2 + (1 - core)
+        for d in (0, 2, 1, 3) if relay else range(groups):
+            o = source(d, 1 - core) * 2 + (1 - core)
             remote(
                 af.at[step, :, block(o)], af.at[step, :, block(o)], fw_s.at[step, d], fw_r.at[step, d], partner, me_s
             ).wait_recv()
@@ -388,7 +411,7 @@
         lax.fori_loop(0, xb // xc, rows, 0)
 
     none = jnp.zeros((zb, ny), F32)
-    order_d = list(range(1, groups)) + [0]
+    order_d = [3, 1, 2, 0] if relay else list(range(1, groups)) + [0]
     gather_fields(0, a_ref)
     lax.fori_loop(0, n_orb, load_start, 0)
     for step in range(STEPS):
@@ -404,12 +427,10 @@
             )
             t, tn = tn, t
 
-        def last(j, acc):
-            side, d = j // groups, lax.rem(j % groups + 1, groups)
-            other = side + core - 2 * side * core
-            return term_block(step, TERMS, t, tn, group(d) * 2 + 1 - other, acc)
-
-        norm_tile = lax.fori_loop(0, n_orb, last, none)
+        norm_tile = none
+        for c in (1 - core, core):
+            for d in order_d:
+                norm_tile = term_block(step, TERMS, t, tn, group(d, c) * 2 + c, norm_tile)
         nbs[step] = norm_tile
         for d in range(1, n_slab):
             c = remote(
@@ -418,7 +439,7 @@
             c.start()
             sends.append(c)
         for d in order_d:
-            current(step, group(d) * 2 + (1 - core), None, jmine.at[d])
+            current(step, group(d, 1 - core) * 2 + (1 - core), None, jmine.at[d])
         for d in range(1, n_slab):
             remote(nbs.at[step], nbr.at[step, d], nb_s.at[step, d], nb_r.at[step, d], me, me_s).wait_recv()
             norm_tile = norm_tile + nbr[step, d]
@@ -438,11 +459,19 @@
             remote(
                 jsend.at[step, d], prx.at[step, d], pr_s.at[step, d], pr_r.at[step, d], partner, me_s
             ).wait_recv()
+            if relay and d == 2:
+                remote(
+                    jsum.at[step, 3], rsx.at[step, 3], rs_s.at[step, 3], rs_r.at[step, 3], partner, me_s
+                ).wait_recv()
             for comp in range(3):
-                jsum[step, d, comp] = jmine[d, comp] + prx[step, d, comp]
+                total = jmine[d, comp] + prx[step, d, comp]
+                if relay and d == 2:
+                    total = total + rsx[step, 3, comp]
+                jsum[step, d, comp] = total
             if d:
+                to = group(1 if relay and d == 3 else d) * 2 + core
                 c = remote(
-                    jsum.at[step, d], rsx.at[step, d], rs_s.at[step, d], rs_r.at[step, d], group(d) * 2 + core, me_s
+                    jsum.at[step, d], rsx.at[step, d], rs_s.at[step, d], rs_r.at[step, d], to, me_s
                 )
                 c.start()
                 sends.append(c)
@@ -463,14 +492,15 @@
             for side in range(2):
                 for part in range(2):
                     hz[base + TERMS + 1, side, part] = scale[0:1] * hs[side, part]
-        for d in range(1, groups):
+        arriving = range(1, 3 if relay else groups)
+        for d in arriving:
             remote(
                 jsum.at[step, d], rsx.at[step, d], rs_s.at[step, d], rs_r.at[step, d], partner, me_s
             ).wait_recv()
 
         for comp in range(3):
             flow = jsum[step, 0, comp]
-            for d in range(1, groups):
+            for d in arriving:
                 flow = flow + rsx[step, d, comp]
             if step == STEPS - 1:
                 half_ref[comp] = enew[step, comp]

time: 98.8 us -> 94.7 us (0.959)
  Pallas kernels: 92.4 us -> 88.3 us
    pallas_call x1, Pallas kernels: 92.4 us -> 88.3 us  [per_device(): pl.pallas_call(functools.partial(kernel, n_orb, n_slab), out_shape=(jax.S...]
where the time goes in v3:
time: 94.7 us; the launch traced here: 94.4 us
  Pallas kernels  88.3 us (93%)
  other arithmetic  4.16 us (4%)
  between operations  1.29 us (1%)
    pallas_call x1, Pallas kernels, per_device(): pl.pallas_call(functools.partial(kernel, n_orb, n_slab), out_shape=(jax.S...  88.3 us
    mul x1, other arithmetic, per_device(): return (moved * scale, e_next, a_old - wave_step * e_next)  2.26 us
    sub x1, other arithmetic, per_device(): return (moved * scale, e_next, a_old - wave_step * e_next)  1.89 us

profile of v3, /device:TPU:0, one launch (start us, length us, event | category | flops | bytes accessed | tf_op | source)
XLA Modules:
  0.0 94.4 jit_solution(9719080963821339818)
XLA Ops:
  1.3 88.3 %shard_map.76 = (f32[1,2,128,8,128]{4,3,2,1,0:T(8,128)}, f32[8,128]{1,0:T(8,128)}, f32[3,16,8,128]{3,2,1,0:T(8,128)}, f32[3,16,8,128]{3,2,1,0:T(8,128)}, f32[3,16,8,128]{3,2,1,0:T(8,128)}) custom-call(f32[1,2,128,8,128]{4,3,2,1,0:T(8,128)} %orb_ref.1, f32[128,8,128]{2,1,0:T(8,128)} %pot_ref.1, f32[1]{0:T(128)S(6)} %copy.8.occ_ref, f32[3,16,8,128]{3,2,1,0:T(8,128)} %e_ref.1, ...), custom_call_target="tpu_custom_call" | custom-call | tf_op jit(solution)/shard_map/pallas_call | solution.py:545
  89.6 1.9 %multiply_subtract_fusion = (f32[3,16,8,128]{3,2,1,0:T(8,128)}, f32[3,16,8,128]{3,2,1,0:T(8,128)}) fusion(f32[3,16,8,128]{3,2,1,0:T(8,128)} %get-tuple-element.12, f32[3,16,8,128]{3,2,1,0:T(8,128)} %get-tuple-element.10, f32[3,16,8,128]{3,2,1,0:T(8,128)} %get-tuple-element.11), kind=kLoop, calls=%fused_computation.1 | loop fusion | flops 196608 | bytes 983040 | tf_op jit(solution)/shard_map/sub | solution.py:597
  91.5 0.0 copy-start
  91.5 0.7 copy-done
  92.2 2.3 %broadcast_multiply_fusion = f32[1,2,128,8,128]{4,3,2,1,0:T(8,128)} fusion(f32[1,2,128,8,128]{4,3,2,1,0:T(8,128)} %get-tuple-element.8, f32[8,128]{1,0:T(8,128)S(1)} %copy-done), kind=kLoop, calls=%fused_computation | loop fusion | flops 262144 | bytes 2101248 | tf_op jit(solution)/shard_map/mul | solution.py:597
Async XLA Ops:
  91.5 0.7 copy-start

commit v4 on v3

--- a/solution.py
+++ b/solution.py
@@ -28,9 +28,8 @@
     a_ref,
     out_ref,
     scale_ref,
-    half_ref,
-    flow_ref,
-    aold_ref,
+    eout_ref,
+    aout_ref,
     ta,
     tb,
     tot,
@@ -183,7 +182,8 @@
             af[step, comp, 0] = zero_x
             af[step, comp, nx + 1] = zero_x
 
-    def load_start(o, carry):
+    def load_start(j, carry):
+        o = lax.rem(me + j, n_orb)
         for i in range(xb // xc):
             x = o * xb + i * xc
             for part in range(2):
@@ -231,8 +231,7 @@
     def finish_gather(step, src, use):
         for comp in range(3):
             af[step, comp, block(me)] = src[comp]
-        weigh(step, me)
-        use(me)
+        pending = me
         for d in (2, 1, 3) if relay else range(1, groups):
             o = source(d) * 2 + core
             remote(
@@ -254,8 +253,11 @@
             )
             c.start()
             sends.append(c)
-            weigh(step, o)
-            use(o)
+            weigh(step, pending)
+            use(pending)
+            pending = o
+        weigh(step, pending)
+        use(pending)
         for d in (0, 2, 1, 3) if relay else range(groups):
             o = source(d, 1 - core) * 2 + (1 - core)
             remote(
@@ -502,14 +504,14 @@
             flow = jsum[step, 0, comp]
             for d in arriving:
                 flow = flow + rsx[step, d, comp]
+            e = enew[step, comp] - wave_step * flow
+            a = a_src[comp] - wave_step * e
             if step == STEPS - 1:
-                half_ref[comp] = enew[step, comp]
-                flow_ref[comp] = flow
-                aold_ref[comp] = a_src[comp]
+                eout_ref[comp] = e
+                aout_ref[comp] = a
             else:
-                e = enew[step, comp] - wave_step * flow
                 ekeep[comp] = e
-                anew[step, comp] = a_src[comp] - wave_step * e
+                anew[step, comp] = a
         if step < STEPS - 1:
             gather_fields(step + 1, anew.at[step])
         else:
@@ -542,17 +544,16 @@
     def buf(*shape):
         return pltpu.VMEM(shape, F32)
 
-    moved, scale, half, flow, a_old = pl.pallas_call(
+    moved, scale, e_next, a_next = pl.pallas_call(
         functools.partial(kernel, n_orb, n_slab),
         out_shape=(
             jax.ShapeDtypeStruct(orbitals.shape, F32),
             jax.ShapeDtypeStruct((zb, ny), F32),
             jax.ShapeDtypeStruct(e_field.shape, F32),
             jax.ShapeDtypeStruct(e_field.shape, F32),
-            jax.ShapeDtypeStruct(e_field.shape, F32),
         ),
         in_specs=[vmem, vmem, pl.BlockSpec(memory_space=pltpu.SMEM), vmem, vmem],
-        out_specs=(vmem,) * 5,
+        out_specs=(vmem,) * 4,
         scratch_shapes=[
             buf(2, nx + 2, zb, ny),
             buf(2, nx + 2, zb, ny),
@@ -593,8 +594,7 @@
             collective_id=0, has_side_effects=True, vmem_limit_bytes=60 * 1024 * 1024
         ),
     )(orbitals, potential, occupation, e_field, a_field)
-    e_next = half - wave_step * flow
-    return (moved * scale, e_next, a_old - wave_step * e_next)
+    return (moved * scale, e_next, a_next)
 
 
 def solution(mesh):

time: 94.7 us -> 95.2 us (level)
  other arithmetic: 4.16 us -> 2.3 us
  local copies, waits for them, and re-layouts: 0.68 us -> 2.34 us
    sub x1 -> x0, other arithmetic: 1.89 us -> none  [per_device(): return (moved * scale, e_next, a_old - wave_step * e_next)]
    unnamed x2 -> x8, local copies, waits for them, and re-layouts: 0.68 us -> 2.34 us
where the time goes in v4:
time: 95.2 us; the launch traced here: 95 us
  Pallas kernels  89.1 us (94%)
  local copies, waits for them, and re-layouts  2.34 us (2%)
  other arithmetic  2.3 us (2%)
  between operations  1.3 us (1%)
    pallas_call x1, Pallas kernels, per_device(): pl.pallas_call(functools.partial(kernel, n_orb, n_slab), out_shape=(jax.S...  89.1 us
    unnamed x8, local copies, waits for them, and re-layouts  2.34 us
    mul x1, other arithmetic, per_device(): return (moved * scale, e_next, a_next)  2.3 us

profile of v4, /device:TPU:0, one launch (start us, length us, event | category | flops | bytes accessed | tf_op | source)
XLA Modules:
  0.0 95.0 jit_solution(9689180956820655745)
XLA Ops:
  1.3 89.1 %shard_map.76 = (f32[1,2,128,8,128]{4,3,2,1,0:T(8,128)}, f32[8,128]{1,0:T(8,128)}, f32[3,16,8,128]{3,2,1,0:T(8,128)}, f32[3,16,8,128]{3,2,1,0:T(8,128)}) custom-call(f32[1,2,128,8,128]{4,3,2,1,0:T(8,128)} %orb_ref.1, f32[128,8,128]{2,1,0:T(8,128)} %pot_ref.1, f32[1]{0:T(128)S(6)} %copy.10.occ_ref, f32[3,16,8,128]{3,2,1,0:T(8,128)} %e_ref.1, ...), custom_call_target="tpu_custom_call" | custom-call | tf_op jit(solution)/shard_map/pallas_call | solution.py:547
  90.3 0.0 copy-start.2
  90.4 0.7 copy-done.2
  91.0 0.0 copy-start.1
  91.0 2.3 %broadcast_multiply_fusion = f32[1,2,128,8,128]{4,3,2,1,0:T(8,128)} fusion(f32[1,2,128,8,128]{4,3,2,1,0:T(8,128)} %get-tuple-element.7, f32[8,128]{1,0:T(8,128)S(1)} %copy-done.2), kind=kLoop, calls=%fused_computation | loop fusion | flops 262144 | bytes 2101248 | tf_op jit(solution)/shard_map/mul | solution.py:597
  93.3 0.0 copy-done.1
  93.3 0.0 copy-start
  93.3 0.7 copy.11
  94.0 0.3 copy-done
  94.3 0.7 copy.12
Async XLA Ops:
  90.3 0.7 copy-start.2
  91.0 2.3 %copy-start.1 = (f32[3,16,8,128]{3,2,1,0:T(8,128)S(1)}, f32[3,16,8,128]{3,2,1,0:T(8,128)}, u32[]{:S(2)}) copy-start(f32[3,16,8,128]{3,2,1,0:T(8,128)} %get-tuple-element.15) | copy-start | bytes 589828
  93.3 1.0 %copy-start = (f32[3,16,8,128]{3,2,1,0:T(8,128)S(1)}, f32[3,16,8,128]{3,2,1,0:T(8,128)}, u32[]{:S(2)}) copy-start(f32[3,16,8,128]{3,2,1,0:T(8,128)} %get-tuple-element.16) | copy-start | bytes 589828
